TPU v7x, 32 devices: a whole 2x2x4 slice. The times are simulated.
32 devices in a mesh: dp: 4 (over y, core), ep: 8 (over z, x).
Axes of the slice: x: 2, y: 2, z: 4, core: 2. Of those that a mesh axis runs over, the one named last changes fastest.
Arguments:
- tokens: bfloat16 [32, 256, 2048], P(('dp', 'ep')), may hold values from -6 to 6
- lengths: int32 [32], P(('dp', 'ep')), may hold values from 64 to 256, as said below
- routes: int32 [32, 256, 8], P(('dp', 'ep')), may hold values from 0 to 15, all different within a row
- pair_order: int32 [32, 2048], P(('dp', 'ep')), may hold values from 0 to 2047, each once within a row
- gate_weights: float32 [32, 256, 8], P(('dp', 'ep')), may hold values from 0.05 to 0.5
- attn_weight: bfloat16 [2048, 8192], P(('dp', 'ep')), may hold values from -0.375 to 0.375
- gains: float32 [4352], replicated, may hold values from 0.5 to 1.5
- expert_gate_up: bfloat16 [16, 2048, 2048], P('ep'), may hold values from -0.125 to 0.125
- expert_down: bfloat16 [16, 1024, 2048], P('ep'), may hold values from -0.375 to 0.375
- cotangent: bfloat16 [32, 256, 2048], P(('dp', 'ep')), may hold values from -6 to 6
Outputs:
- output: bfloat16 [32, 256, 2048], P(('dp', 'ep'))
- input_grad: float32 [32, 256, 2048], P(('dp', 'ep'))
- attn_weight_grad: float32 [2048, 8192], P(('dp', 'ep'))
- gains_grad: float32 [4352], P(('dp', 'ep'))
- gate_up_grad: float32 [16, 2048, 2048], P('ep', 'dp')
- down_grad: float32 [16, 1024, 2048], P('ep', 'dp')
Inputs may be any that keep to these rules, and one draw needn't show every extreme that they name: `lengths`: slots at or beyond a sequence's length are padding; in every draw some sequence fills all 256 slots. `routes`: the 8 experts of a slot are distinct. `pair_order`: within each sequence every value appears once.
All inputs are finite; a program needn't handle non-finite values.
Results may differ from a plain program's by a relative error of at most 0.014.
Values may be sent and summed in bfloat16 or wider, within the bound.
No kernel may reach another device: no remote copies, remote signals or barrier semaphores. Data moves between devices by JAX's collectives and lax.ppermute only.
A program may use at most 448 MiB of HBM per device.

v0:
```python
import math

import jax
import jax.numpy as jnp
from jax import lax
from jax.sharding import PartitionSpec as P

HEAD = 128


EPS = 1e-06
THETA = 10000.0
NEG = -1e30


def inv_rms(values):
    return lax.rsqrt(jnp.mean(values * values, axis=-1, keepdims=True) + EPS)


def norm_back(values, inv_scale, gain_vec, grad_in):
    scaled = grad_in * gain_vec
    mean_term = jnp.mean(scaled * values, axis=-1, keepdims=True)
    return inv_scale * scaled - values * (inv_scale * inv_scale * inv_scale) * mean_term


def rope_tables(slot_count, head_size):
    half_size = head_size // 2
    frequency = THETA ** (-(jnp.arange(half_size, dtype=jnp.float32) * 2.0) / head_size)
    angles = jnp.arange(slot_count, dtype=jnp.float32)[:, None] * frequency[None, :]
    return (jnp.cos(angles)[:, None, :], jnp.sin(angles)[:, None, :])


def rotary(values, cosine_table, sine_table):
    half_size = values.shape[-1] // 2
    first_half = values[..., :half_size]
    second_half = values[..., half_size:]
    return jnp.concatenate(
        [
            first_half * cosine_table - second_half * sine_table,
            second_half * cosine_table + first_half * sine_table,
        ],
        axis=-1,
    )


def rotary_back(grad_in, cosine_table, sine_table):
    half_size = grad_in.shape[-1] // 2
    first_half = grad_in[..., :half_size]
    second_half = grad_in[..., half_size:]
    return jnp.concatenate(
        [
            first_half * cosine_table + second_half * sine_table,
            second_half * cosine_table - first_half * sine_table,
        ],
        axis=-1,
    )


def on_device(
    tokens,
    lengths,
    routes,
    pair_order,
    gate_weights,
    attn_weight,
    gains,
    expert_gate_up,
    expert_down,
    cotangent,
):
    slot_count = tokens.shape[1]
    model_width = tokens.shape[2]
    head_size = HEAD
    head_count = model_width // head_size
    top_count = routes.shape[2]
    experts_dev = expert_gate_up.shape[0]
    hidden_units = expert_down.shape[1]
    groups = lax.axis_size("ep")
    experts = experts_dev * groups
    capacity = (9 * slot_count * top_count + 8 * experts - 1) // (8 * experts)
    pair_count = slot_count * top_count
    factor = 1.0 / math.sqrt(head_size)
    inputs = tokens[0].astype(jnp.float32)
    length = lengths[0]
    slot_live = jnp.arange(slot_count) < length
    live_rows = slot_live.astype(jnp.float32)[:, None]
    gain_attn = gains[:model_width]
    gain_ffn = gains[model_width : 2 * model_width]
    gain_query = gains[2 * model_width : 2 * model_width + head_size]
    gain_key = gains[2 * model_width + head_size :]
    whole_weight = lax.all_gather(attn_weight, ("dp", "ep"), axis=0, tiled=True)
    weight_qkv = whole_weight[:, : 3 * model_width]
    weight_out = whole_weight[:, 3 * model_width :]
    scale_first = inv_rms(inputs)
    xn_first = (inputs * scale_first * gain_attn).astype(jnp.bfloat16)
    projected = jnp.dot(xn_first, weight_qkv, preferred_element_type=jnp.float32)
    query_raw = projected[:, :model_width].reshape(slot_count, head_count, head_size)
    key_raw = projected[:, model_width : 2 * model_width].reshape(slot_count, head_count, head_size)
    values_low = (
        projected[:, 2 * model_width :]
        .astype(jnp.bfloat16)
        .reshape(slot_count, head_count, head_size)
    )
    cosine_table, sine_table = rope_tables(slot_count, head_size)
    query_scale = inv_rms(query_raw)
    key_scale = inv_rms(key_raw)
    query_rot = rotary(query_raw * query_scale * gain_query, cosine_table, sine_table).astype(
        jnp.bfloat16
    )
    key_rot = rotary(key_raw * key_scale * gain_key, cosine_table, sine_table).astype(jnp.bfloat16)

    def score_table():
        raw_scores = (
            jnp.einsum("qhd,khd->hqk", query_rot, key_rot, preferred_element_type=jnp.float32)
            * factor
        )
        return jnp.where(slot_live[None, None, :], raw_scores, NEG)

    scores = score_table()
    row_max = jnp.max(scores, axis=-1, keepdims=True)
    log_total = row_max + jnp.log(jnp.sum(jnp.exp(scores - row_max), axis=-1, keepdims=True))
    probs_low = jnp.exp(scores - log_total).astype(jnp.bfloat16)
    attended = jnp.einsum("hqk,khd->qhd", probs_low, values_low, preferred_element_type=jnp.float32)
    attended = attended.reshape(slot_count, model_width).astype(jnp.bfloat16)
    resid = inputs + jnp.dot(attended, weight_out, preferred_element_type=jnp.float32)
    scale_second = inv_rms(resid)
    xn_second = (resid * scale_second * gain_ffn).astype(jnp.bfloat16)
    expert_flat = routes[0].reshape(pair_count)
    order_row = pair_order[0]
    pair_index = jnp.arange(pair_count, dtype=jnp.int32)
    pair_live = pair_index // top_count < length
    by_rank = jnp.zeros((pair_count,), jnp.int32).at[order_row].set(pair_index)
    one_hot = (
        (expert_flat[by_rank][:, None] == jnp.arange(experts, dtype=jnp.int32)[None, :])
        & pair_live[by_rank][:, None]
    ).astype(jnp.int32)
    earlier = jnp.cumsum(one_hot, axis=0) - one_hot
    pair_rank = jnp.sum(earlier * one_hot, axis=1)[order_row]
    kept_pair = pair_live & (pair_rank < capacity)
    dest_slot = jnp.where(kept_pair, expert_flat * capacity + pair_rank, experts * capacity)
    source = (
        jnp.full((experts * capacity + 1,), pair_count, jnp.int32).at[dest_slot].set(pair_index)
    )
    source = source[: experts * capacity]
    source_token = source // top_count
    xn_ext = jnp.concatenate([xn_second, jnp.zeros((1, model_width), jnp.bfloat16)], axis=0)
    send_rows = xn_ext[source_token].reshape(groups, experts_dev, capacity, model_width)
    received = lax.all_to_all(send_rows, "ep", split_axis=0, concat_axis=0, tiled=True)
    gate_up = jnp.einsum(
        "sjcd,jdf->sjcf", received, expert_gate_up, preferred_element_type=jnp.float32
    )
    activation = (jax.nn.silu(gate_up[..., :hidden_units]) * gate_up[..., hidden_units:]).astype(
        jnp.bfloat16
    )
    result = jnp.einsum(
        "sjcf,jfd->sjcd", activation, expert_down, preferred_element_type=jnp.float32
    )
    returned = lax.all_to_all(
        result.astype(jnp.bfloat16), "ep", split_axis=0, concat_axis=0, tiled=True
    )
    returned, received, gate_up, activation = (returned, received, gate_up, activation)
    back_ext = jnp.concatenate(
        [
            returned.reshape(experts * capacity, model_width),
            jnp.zeros((1, model_width), jnp.bfloat16),
        ],
        axis=0,
    )
    weight = jnp.where(kept_pair, gate_weights[0].reshape(pair_count), 0.0)
    mixed = jnp.sum(
        (back_ext[dest_slot].astype(jnp.float32) * weight[:, None]).reshape(
            slot_count, top_count, model_width
        ),
        axis=1,
    )
    output = (live_rows * (resid + mixed)).astype(jnp.bfloat16)
    grad_out = cotangent[0].astype(jnp.float32) * live_rows
    grad_ext = jnp.concatenate([grad_out, jnp.zeros((1, model_width), jnp.float32)], axis=0)
    weight_ext = jnp.concatenate([weight, jnp.zeros((1,), jnp.float32)], axis=0)
    slot_grad = (grad_ext[source_token] * weight_ext[source][:, None]).astype(jnp.bfloat16)
    slot_grad = slot_grad.reshape(groups, experts_dev, capacity, model_width)
    grad_recv = lax.all_to_all(slot_grad, "ep", split_axis=0, concat_axis=0, tiled=True)
    grad_act = jnp.einsum(
        "sjcd,jfd->sjcf", grad_recv, expert_down, preferred_element_type=jnp.float32
    )
    grad_down = jnp.einsum(
        "sjcf,sjcd->jfd", activation, grad_recv, preferred_element_type=jnp.float32
    )
    gate_part = gate_up[..., :hidden_units]
    up_part = gate_up[..., hidden_units:]
    sigmoid_gate = jax.nn.sigmoid(gate_part)
    grad_gate = grad_act * up_part * sigmoid_gate * (1.0 + gate_part * (1.0 - sigmoid_gate))
    grad_up = grad_act * gate_part * sigmoid_gate
    grad_gate_up = jnp.concatenate([grad_gate, grad_up], axis=-1).astype(jnp.bfloat16)
    grad_weight_gu = jnp.einsum(
        "sjcd,sjcf->jdf", received, grad_gate_up, preferred_element_type=jnp.float32
    )
    grad_rows = jnp.einsum(
        "sjcf,jdf->sjcd", grad_gate_up, expert_gate_up, preferred_element_type=jnp.float32
    )
    rows_back = lax.all_to_all(
        grad_rows.astype(jnp.bfloat16), "ep", split_axis=0, concat_axis=0, tiled=True
    )
    rows_ext = jnp.concatenate(
        [
            rows_back.reshape(experts * capacity, model_width),
            jnp.zeros((1, model_width), jnp.bfloat16),
        ],
        axis=0,
    )
    grad_xn_second = jnp.sum(
        rows_ext[dest_slot].astype(jnp.float32).reshape(slot_count, top_count, model_width), axis=1
    )
    expert_sums = (
        lax.psum_scatter(grad_weight_gu, "dp", scatter_dimension=1, tiled=True),
        lax.psum_scatter(grad_down, "dp", scatter_dimension=1, tiled=True),
    )
    grad_resid = grad_out + norm_back(resid, scale_second, gain_ffn, grad_xn_second)
    grad_gain_ffn = jnp.sum(grad_xn_second * resid * scale_second, axis=0)
    grad_branch = grad_resid.astype(jnp.bfloat16)
    grad_wout = jnp.einsum("sa,sb->ab", attended, grad_branch, preferred_element_type=jnp.float32)
    grad_att = jnp.einsum("sb,ab->sa", grad_branch, weight_out, preferred_element_type=jnp.float32)
    grad_att = grad_att.astype(jnp.bfloat16).reshape(slot_count, head_count, head_size)
    scores_again = score_table()
    probs_again = jnp.exp(scores_again - log_total)
    grad_probs = jnp.einsum(
        "qhd,khd->hqk", grad_att, values_low, preferred_element_type=jnp.float32
    )
    grad_values = jnp.einsum(
        "hqk,qhd->khd",
        probs_again.astype(jnp.bfloat16),
        grad_att,
        preferred_element_type=jnp.float32,
    )
    grad_values = grad_values.astype(jnp.bfloat16)
    inner_sum = jnp.sum(probs_again * grad_probs, axis=-1, keepdims=True)
    grad_scores = (probs_again * (grad_probs - inner_sum)).astype(jnp.bfloat16)
    grad_qrot = (
        jnp.einsum("hqk,khd->qhd", grad_scores, key_rot, preferred_element_type=jnp.float32)
        * factor
    )
    grad_krot = (
        jnp.einsum("hqk,qhd->khd", grad_scores, query_rot, preferred_element_type=jnp.float32)
        * factor
    )
    grad_qnorm = rotary_back(grad_qrot, cosine_table, sine_table)
    grad_knorm = rotary_back(grad_krot, cosine_table, sine_table)
    grad_query = norm_back(query_raw, query_scale, gain_query, grad_qnorm).astype(jnp.bfloat16)
    grad_key = norm_back(key_raw, key_scale, gain_key, grad_knorm).astype(jnp.bfloat16)
    grad_gain_query = jnp.sum(grad_qnorm * query_raw * query_scale, axis=(0, 1))
    grad_gain_key = jnp.sum(grad_knorm * key_raw * key_scale, axis=(0, 1))
    grad_proj = jnp.concatenate(
        [
            grad_query.reshape(slot_count, model_width),
            grad_key.reshape(slot_count, model_width),
            grad_values.reshape(slot_count, model_width),
        ],
        axis=1,
    )
    grad_wqkv = jnp.einsum("sa,sb->ab", xn_first, grad_proj, preferred_element_type=jnp.float32)
    grad_xn_first = jnp.einsum(
        "sb,ab->sa", grad_proj, weight_qkv, preferred_element_type=jnp.float32
    )
    input_grad = grad_resid + norm_back(inputs, scale_first, gain_attn, grad_xn_first)
    grad_gain_attn = jnp.sum(grad_xn_first * inputs * scale_first, axis=0)
    gain_terms = jnp.concatenate(
        [grad_gain_attn, grad_gain_ffn, grad_gain_query, grad_gain_key], axis=0
    )
    full_terms = jnp.concatenate([grad_wqkv, grad_wout], axis=1)
    attn_share, gain_share = (
        lax.psum_scatter(full_terms, ("dp", "ep"), scatter_dimension=0, tiled=True),
        lax.psum_scatter(gain_terms, ("dp", "ep"), scatter_dimension=0, tiled=True),
    )
    return (output[None], input_grad[None], attn_share, gain_share, expert_sums[0], expert_sums[1])


def solution(mesh):
    in_specs = (
        P(("dp", "ep"), None, None),
        P(("dp", "ep")),
        P(("dp", "ep"), None, None),
        P(("dp", "ep"), None),
        P(("dp", "ep"), None, None),
        P(("dp", "ep"), None),
        P(),
        P("ep", None, None),
        P("ep", None, None),
        P(("dp", "ep"), None, None),
    )
    out_specs = (
        P(("dp", "ep"), None, None),
        P(("dp", "ep"), None, None),
        P(("dp", "ep"), None),
        P(("dp", "ep")),
        P("ep", "dp", None),
        P("ep", "dp", None),
    )
    return jax.shard_map(
        on_device, mesh=mesh, in_specs=in_specs, out_specs=out_specs, check_vma=False
    )
```

profile of v0, /device:TPU:0, one launch (start us, length us, event | category | flops | bytes accessed | tf_op | source)
XLA Modules:
  0.0 2815.4 jit_solution(5414634431829395121)
XLA Ops:
  11.2 8.0 scatter_custom_fusion
  19.2 13.1 gather_fusion.1
  32.3 11.8 gather_fusion
  44.2 4.6 reduce-window.6
  49.5 11.8 gather_fusion.2
  61.4 8.1 scatter_custom_fusion.1
  73.3 135.3 %all-gather.2.cloned.1.call-done = bf16[2048,8192]{1,0:T(8,128)(2,1)} async-done(((bf16[64,8192]{1,0:T(8,128)(2,1)}), bf16[2048,8192]{1,0:T(8,128)(2,1)}) %all-gather.2.cloned.1.call-update) | async-done | bytes 33554448 | tf_op jit(solution)/shard_map/all_gather | solution.py:91
  208.5 11.7 fusion.2
  220.3 3.4 slice_bitcast_fusion.3
  242.6 6.2 multiply_reduce_fusion.3
  250.2 9.8 gather_fusion.3
  260.0 5.2 all-to-all-start
  266.1 12.3 gather_fusion.6
  279.1 11.5 gather_fusion.5
  290.6 9.9 multiply_convert_fusion
  300.5 171.0 %all-to-all-done = bf16[8,2,144,2048]{3,2,1,0:T(8,128)(2,1)} async-done(((bf16[8,2,144,2048]{3,2,1,0:T(8,128)(2,1)}), bf16[8,2,144,2048]{3,2,1,0:T(8,128)(2,1)}, u32[]{:S(2)}, u32[]{:S(2)}) %all-to-all-start) | async-done | bytes 9437216 | tf_op jit(solution)/shard_map/all_to_all | solution.py:148
  471.5 5.1 all-to-all-start.2
  476.6 27.8 fusion.27
  504.4 177.6 %all-to-all-done.2 = bf16[8,2,144,2048]{3,2,1,0:T(8,128)(2,1)} async-done(((bf16[8,2,144,2048]{3,2,1,0:T(8,128)(2,1)}), bf16[8,2,144,2048]{3,2,1,0:T(8,128)(2,1)}, u32[]{:S(2)}, u32[]{:S(2)}) %all-to-all-start.2) | async-done | bytes 9437216 | tf_op jit(solution)/shard_map/all_to_all | solution.py:182
  682.0 22.7 fusion.11
  704.7 18.3 fusion.32
  723.0 30.6 %convolution_bitcast_fusion = f32[2,2048,2048]{2,1,0:T(8,128)} fusion(bf16[8,2,144,2048]{3,2,1,0:T(8,128)(2,1)} %all-to-all-done, bf16[8,2,144,1024]{3,2,0,1:T(8,128)(2,1)} %get-tuple-element.15, bf16[8,2,144,1024]{3,2,0,1:T(8,128)(2,1)} %get-tuple-element.14), kind=kOutput, calls=%fused_computation.23 | convolution fusion | flops 19346227200 | bytes 52428800 | tf_op jit(solution)/shard_map/sjcd,sjcf->jdf/dot_general | solution.py:195
  753.7 17.2 convert_bitcast_fusion.1
  770.8 9.3 copy.197
  780.1 5.3 all-to-all-start.1
  785.4 25.9 convert_bitcast_fusion
  811.3 9.3 copy.202
  820.6 169.2 %all-to-all-done.1 = bf16[8,2,144,2048]{3,2,1,0:T(8,128)(2,1)} async-done(((bf16[8,2,144,2048]{3,2,1,0:T(8,128)(2,1)}), bf16[8,2,144,2048]{3,2,1,0:T(8,128)(2,1)}, u32[]{:S(2)}, u32[]{:S(2)}) %all-to-all-start.1) | async-done | bytes 9437216 | tf_op jit(solution)/shard_map/all_to_all | solution.py:158
  989.9 5.1 all-to-all-start.3
  997.8 9.3 concatenate.49
  1007.0 192.4 %all-to-all-done.3 = bf16[8,2,144,2048]{3,2,1,0:T(8,128)(2,1)} async-done(((bf16[8,2,144,2048]{3,2,1,0:T(8,128)(2,1)}), bf16[8,2,144,2048]{3,2,1,0:T(8,128)(2,1)}, u32[]{:S(2)}, u32[]{:S(2)}) %all-to-all-start.3) | async-done | bytes 9437216 | tf_op jit(solution)/shard_map/all_to_all | solution.py:201
  1199.4 9.2 concatenate.53
  1208.7 21.3 gather_fusion.4
  1229.9 21.6 gather_fusion.7
  1251.6 11.4 convert_reduce_fusion
  1266.3 12.7 fusion.4
  1279.1 4.1 subtract_add_fusion
  1284.5 5.7 fusion.42
  1296.0 4.3 multiply_reduce_fusion
  1310.5 4.9 fusion.74
  1316.1 9.9 fusion.76
  1331.3 9.0 fusion.61
  1340.3 21.3 fusion.66
  1361.6 43.4 %pad_maximum_fusion = f32[2048,8192]{1,0:T(8,128)} fusion(f32[2048,2048]{1,0:T(8,128)} %fusion.76, f32[2048,6144]{1,0:T(8,128)} %fusion.66), kind=kLoop, calls=%fused_computation.10 | loop fusion | flops 16777216 | bytes 134217728 | tf_op jit(solution)/shard_map/concatenate | solution.py:269
  1405.1 14.7 fusion.55
  1419.9 47.2 %all-reduce.4 = f32[4352]{0:T(1024)S(1)} all-reduce(f32[4352]{0:T(1024)S(1)} %pad_maximum_fusion.13), channel_id=3, replica_groups=mesh['dp'=4,'ep'=8] {'dp','ep'}, use_global_device_ids=true, to_apply=%region_25.26.clone | all-reduce | flops 4352 | bytes 34816
  1467.7 3.5 fusion.52
  1471.2 1337.2 %reduce-scatter.4.cloned.1.call-done = f32[64,8192]{1,0:T(8,128)} async-done(((f32[2048,8192]{1,0:T(8,128)}), f32[64,8192]{1,0:T(8,128)}) %reduce-scatter.4.cloned.1.call-update) | async-done | bytes 2097168 | tf_op jit(solution)/shard_map/reduce_scatter | solution.py:271
  (240 shorter events, 59.4 us)
Async XLA Ops:
  7.2 201.4 %all-gather.2.cloned.1.call-start = ((), (), s32[]{:S(2)}) async-start(), calls=%async_computation.7 | async-start | bytes 34603008 | tf_op jit(solution)/shard_map/all_gather | solution.py:91
  49.5 21.2 copy-start.9
  49.5 22.0 copy-start.61
  61.3 147.2 %copy-start.43 = (s32[2048]{0:T(1024)}, s32[2048]{0:T(1024)S(1)}, u32[]{:S(2)}) copy-start(s32[2048]{0:T(1024)S(1)} %gather_fusion.2) | copy-start | bytes 24580
  61.4 10.2 copy-start.55
  71.6 137.0 %copy-start.45 = (f32[256]{0:T(256)}, f32[256]{0:T(256)S(1)}, u32[]{:S(2)}) copy-start(f32[256]{0:T(256)S(1)} %get-tuple-element.52) | copy-start | bytes 3076
  72.8 135.8 %copy-start.29 = (f32[2048]{0:T(1024)}, f32[2048]{0:T(1024)S(1)}, u32[]{:S(2)}) copy-start(f32[2048]{0:T(1024)S(1)} %get-tuple-element.42) | copy-start | bytes 24580
  73.3 161.2 %copy-start.25 = (f32[256,64]{1,0:T(8,128)}, f32[256,64]{1,0:T(8,128)S(1)}, u32[]{:S(2)}) copy-start(f32[256,64]{1,0:T(8,128)S(1)} %get-tuple-element.55) | copy-start | bytes 196612
  73.3 161.2 %copy-start.27 = (f32[256,64]{1,0:T(8,128)}, f32[256,64]{1,0:T(8,128)S(1)}, u32[]{:S(2)}) copy-start(f32[256,64]{1,0:T(8,128)S(1)} %get-tuple-element.56) | copy-start | bytes 196612
  224.1 7.6 copy-start.5
  227.1 4.6 copy-start.36
  242.6 6.2 copy-start.21
  242.6 6.9 copy-start.40
  260.0 5.2 copy-start.53
  260.0 5.5 copy-start.44
  260.0 6.1 copy-start.49
  260.0 211.5 %all-to-all-start = ((bf16[8,2,144,2048]{3,2,1,0:T(8,128)(2,1)}), bf16[8,2,144,2048]{3,2,1,0:T(8,128)(2,1)}, u32[]{:S(2)}, u32[]{:S(2)}) async-start(bf16[8,2,144,2048]{3,2,1,0:T(8,128)(2,1)} %bitcast.234), calls=%async_computation | async-start | bytes 18874368 | tf_op jit(solution)/shard_map/all_to_all | solution.py:148
  266.1 12.4 copy-start.23
  266.1 12.4 copy-start.62
  471.5 210.5 %all-to-all-start.2 = ((bf16[8,2,144,2048]{3,2,1,0:T(8,128)(2,1)}), bf16[8,2,144,2048]{3,2,1,0:T(8,128)(2,1)}, u32[]{:S(2)}, u32[]{:S(2)}) async-start(bf16[8,2,144,2048]{3,2,1,0:T(8,128)(2,1)} %multiply_convert_fusion), calls=%async_computation.2 | async-start | bytes 18874368 | tf_op jit(solution)/shard_map/all_to_all | solution.py:182
  476.6 994.7 %reduce-scatter.8.cloned.1.call-start = ((), (), s32[]{:S(2)}) async-start(), calls=%async_computation.10 | async-start | bytes 20971520 | tf_op jit(solution)/shard_map/reduce_scatter | solution.py:216
  723.0 748.3 %reduce-scatter.6.cloned.1.call-start = ((), (), s32[]{:S(2)}) async-start(), calls=%async_computation.9 | async-start | bytes 41943040 | tf_op jit(solution)/shard_map/reduce_scatter | solution.py:215
  780.1 209.8 %all-to-all-start.1 = ((bf16[8,2,144,2048]{3,2,1,0:T(8,128)(2,1)}), bf16[8,2,144,2048]{3,2,1,0:T(8,128)(2,1)}, u32[]{:S(2)}, u32[]{:S(2)}) async-start(bf16[8,2,144,2048]{3,2,1,0:T(8,128)(2,1)} %copy.197), calls=%async_computation.1 | async-start | bytes 18874368 | tf_op jit(solution)/shard_map/all_to_all | solution.py:158
  820.6 174.5 %copy-start.68 = (pred[2048]{0:T(1024)(128)(4,1)S(1)}, pred[2048]{0:T(1024)(128)(4,1)}, u32[]{:S(2)}) copy-start(pred[2048]{0:T(1024)(128)(4,1)} %get-tuple-element.13) | copy-start | bytes 6148
  820.6 174.7 %copy-start.54 = (f32[1,256,8]{1,2,0:T(8,128)S(1)}, f32[1,256,8]{1,2,0:T(8,128)}, u32[]{:S(2)}) copy-start(f32[1,256,8]{1,2,0:T(8,128)} %param.14) | copy-start | bytes 24580
  820.6 175.5 %copy-start.56 = (s32[2048,1]{0,1:T(1,128)S(1)}, s32[2048,1]{0,1:T(1,128)}, u32[]{:S(2)}) copy-start(s32[2048,1]{0,1:T(1,128)} %copy-done.55) | copy-start | bytes 24580
  820.6 175.5 %copy-start.64 = (f32[128]{0:T(128)S(1)}, f32[128]{0:T(128)}, u32[]{:S(2)}) copy-start(f32[128]{0:T(128)} %get-tuple-element.44) | copy-start | bytes 1540
  820.6 175.5 %copy-start.66 = (f32[128]{0:T(128)S(1)}, f32[128]{0:T(128)}, u32[]{:S(2)}) copy-start(f32[128]{0:T(128)} %get-tuple-element.43) | copy-start | bytes 1540
  820.6 176.1 %copy-start.37 = (f32[256,16]{0,1:T(8,128)S(1)}, f32[256,16]{0,1:T(8,128)}, u32[]{:S(2)}) copy-start(f32[256,16]{0,1:T(8,128)} %copy-done.36) | copy-start | bytes 49156
  820.6 176.2 %copy-start.39 = (f32[256,16]{0,1:T(8,128)S(1)}, f32[256,16]{0,1:T(8,128)}, u32[]{:S(2)}) copy-start(f32[256,16]{0,1:T(8,128)} %copy-done.38) | copy-start | bytes 49156
  820.6 176.3 %copy-start.47 = (f32[256,16]{0,1:T(8,128)S(1)}, f32[256,16]{0,1:T(8,128)}, u32[]{:S(2)}) copy-start(f32[256,16]{0,1:T(8,128)} %get-tuple-element.45) | copy-start | bytes 49156
  820.6 177.0 %copy-start.48 = (f32[256,16]{0,1:T(8,128)S(1)}, f32[256,16]{0,1:T(8,128)}, u32[]{:S(2)}) copy-start(f32[256,16]{0,1:T(8,128)} %get-tuple-element.47) | copy-start | bytes 49156
  989.9 209.5 %all-to-all-start.3 = ((bf16[8,2,144,2048]{3,2,1,0:T(8,128)(2,1)}), bf16[8,2,144,2048]{3,2,1,0:T(8,128)(2,1)}, u32[]{:S(2)}, u32[]{:S(2)}) async-start(bf16[8,2,144,2048]{3,2,1,0:T(8,128)(2,1)} %copy.202), calls=%async_computation.3 | async-start | bytes 18874368 | tf_op jit(solution)/shard_map/all_to_all | solution.py:201
  995.0 1813.4 %reduce-scatter.4.cloned.1.call-start = ((), (), s32[]{:S(2)}) async-start(), calls=%async_computation.8 | async-start | bytes 69206016 | tf_op jit(solution)/shard_map/reduce_scatter | solution.py:271
  1251.6 11.4 copy-start.8
  1251.6 11.4 copy-start.41
  1251.6 11.4 copy-start.60
  1266.3 12.7 copy-start.24
  1266.3 12.7 copy-start.63
  1310.5 5.7 copy-start.22
  1310.5 19.8 slice-start
  1316.1 14.2 slice-start.1
  1331.3 9.0 copy-start.10
  1331.3 9.0 copy-start.30
  1331.3 9.0 copy-start.46
  1405.1 14.8 copy-start.50
  1405.1 62.6 %copy-start.4 = (f32[256,2048]{1,0:T(8,128)S(1)}, f32[256,2048]{1,0:T(8,128)}, u32[]{:S(2)}) copy-start(f32[256,2048]{1,0:T(8,128)} %copy-done.3) | copy-start | bytes 6291460
  1405.1 62.6 %copy-start.69 = (f32[256]{0:T(256)S(1)}, f32[256]{0:T(256)}, u32[]{:S(2)}) copy-start(f32[256]{0:T(256)} %get-tuple-element.51) | copy-start | bytes 3076
  (32 other events, 58.9 us)
Sparse Core Ops, SparseCore 0:
  11.0 197.5 all-gather.1
  723.1 125.1 reduce-scatter.7
  851.6 234.8 reduce-scatter.5
  1405.2 1403.1 reduce-scatter.3
where the time goes:
time: 2820 us
  waiting for transfers between devices  2180 us (77%)
  matrix products  226 us (8%)
  local copies, waits for them, and re-layouts  194 us (7%)
  other arithmetic  128 us (5%)
  blocking collectives  47.2 us (2%)
    reduce_scatter x1, waiting for transfers between devices, on_device(): lax.psum_scatter(full_terms, ('dp', 'ep'), scatter_dimension=0, tiled=True)  1340 us
    all_to_all x1, waiting for transfers between devices, on_device(): lax.all_to_all(grad_rows.astype(jnp.bfloat16), 'ep', split_axis=0, concat...  192 us
    all_to_all x1, waiting for transfers between devices, on_device(): lax.all_to_all(slot_grad, 'ep', split_axis=0, concat_axis=0, tiled=True)  178 us
    all_to_all x1, waiting for transfers between devices, on_device(): lax.all_to_all(send_rows, 'ep', split_axis=0, concat_axis=0, tiled=True)  171 us
    all_to_all x1, waiting for transfers between devices, on_device(): lax.all_to_all(result.astype(jnp.bfloat16), 'ep', split_axis=0, concat_ax...  169 us
    all_gather x1, waiting for transfers between devices, on_device(): whole_weight = lax.all_gather(attn_weight, ('dp', 'ep'), axis=0, tiled=True)  135 us
  transfers between devices with their start and end apart: 8, of which 6 were waited for; matrix products, arithmetic and copies ran while one was open for 16% of the time, Pallas kernels for 0%

commit v1 on v0

v1 whole, which is shorter than its diff:
```python
import math

import jax
import jax.numpy as jnp
from jax import lax
from jax.sharding import PartitionSpec as P

HEAD = 128
EPS = 1e-06
THETA = 10000.0
NEG = -1e30
LOW = jnp.bfloat16
F32 = jnp.float32


def swap(value, axis, mask):
    count = lax.axis_size(axis)
    return lax.ppermute(value, axis, [(i, i ^ mask) for i in range(count)])


def gather_slots(shard, axis):
    slots = {0: shard}
    bit = lax.axis_size(axis) // 2
    while bit:
        for r in sorted(slots):
            slots[r | bit] = swap(slots[r], axis, bit)
        bit //= 2
    return [slots[r] for r in range(lax.axis_size(axis))]


def scatter_slots(parts, axis):
    acc = [part.astype(F32) for part in parts]
    bit = 1
    while bit < lax.axis_size(axis):
        for r in range(0, len(acc), 2 * bit):
            acc[r] = acc[r] + swap(acc[r | bit].astype(LOW), axis, bit).astype(F32)
        bit *= 2
    return acc[0]


def sum_all(value):
    for axis in ("ep", "dp"):
        bit = 1
        while bit < lax.axis_size(axis):
            value = value + swap(value, axis, bit)
            bit *= 2
    return value


def inv_rms(values):
    return lax.rsqrt(jnp.mean(values * values, axis=-1, keepdims=True) + EPS)


def norm_back(values, inv_scale, gain_vec, grad_in):
    scaled = grad_in * gain_vec
    mean_term = jnp.mean(scaled * values, axis=-1, keepdims=True)
    return inv_scale * scaled - values * (inv_scale * inv_scale * inv_scale) * mean_term


def rope_tables(slot_count, head_size):
    half_size = head_size // 2
    frequency = THETA ** (-(jnp.arange(half_size, dtype=F32) * 2.0) / head_size)
    angles = jnp.arange(slot_count, dtype=F32)[:, None] * frequency[None, :]
    return (jnp.cos(angles)[:, None, :], jnp.sin(angles)[:, None, :])


def rotary(values, cosine_table, sine_table):
    half_size = values.shape[-1] // 2
    first_half = values[..., :half_size]
    second_half = values[..., half_size:]
    return jnp.concatenate(
        [
            first_half * cosine_table - second_half * sine_table,
            second_half * cosine_table + first_half * sine_table,
        ],
        axis=-1,
    )


def dot(a, b):
    return jnp.dot(a, b, preferred_element_type=F32)


def on_device(
    tokens,
    lengths,
    routes,
    pair_order,
    gate_weights,
    attn_weight,
    gains,
    expert_gate_up,
    expert_down,
    cotangent,
):
    slot_count, width = tokens.shape[1:]
    top_count = routes.shape[2]
    experts_dev, hidden = expert_down.shape[:2]
    rows_dev = attn_weight.shape[0]
    n_dp, n_ep = lax.axis_size("dp"), lax.axis_size("ep")
    my_dp, my_ep = lax.axis_index("dp"), lax.axis_index("ep")
    experts = experts_dev * n_ep
    capacity = (9 * slot_count * top_count + 8 * experts - 1) // (8 * experts)
    heads_dev = width // HEAD // n_dp
    cols = heads_dev * HEAD
    factor = 1.0 / math.sqrt(HEAD)

    inputs = tokens[0].astype(F32)
    length = lengths[0]
    slot_index = jnp.arange(slot_count)
    slot_live = slot_index < length
    live_rows = slot_live.astype(F32)[:, None]
    gain_attn = gains[:width]
    gain_ffn = gains[width : 2 * width]
    gain_query = gains[2 * width : 2 * width + HEAD]
    gain_key = gains[2 * width + HEAD :]

    blocks = attn_weight[:, : 3 * width].reshape(rows_dev, 3, n_dp, cols)
    qkv_shard = jnp.zeros((n_dp, rows_dev, 3 * cols), LOW)
    for r in range(n_dp):
        piece = lax.dynamic_index_in_dim(blocks, my_dp ^ r, axis=2, keepdims=False)
        piece = piece.reshape(rows_dev, 3 * cols)
        piece = swap(piece, "dp", r) if r else piece
        qkv_shard = lax.dynamic_update_slice(qkv_shard, piece[None], (my_dp ^ r, 0, 0))
    weight_qkv = jnp.zeros((n_dp, n_ep, rows_dev, 3 * cols), LOW)
    for s, shard in enumerate(gather_slots(qkv_shard, "ep")):
        weight_qkv = lax.dynamic_update_slice(weight_qkv, shard[:, None], (0, my_ep ^ s, 0, 0))
    weight_qkv = weight_qkv.reshape(width, 3 * cols)
    weight_out = jnp.zeros((n_ep, rows_dev, width), LOW)
    for s, shard in enumerate(gather_slots(attn_weight[:, 3 * width :], "ep")):
        weight_out = lax.dynamic_update_slice(weight_out, shard[None], (my_ep ^ s, 0, 0))
    weight_out = weight_out.reshape(cols, width)

    named = routes[0][:, :, None] == jnp.arange(experts, dtype=jnp.int32)
    order = pair_order[0].reshape(slot_count, top_count)[:, :, None]
    order_of = jnp.sum(jnp.where(named, order, 0), axis=1).T
    weight_of = jnp.sum(jnp.where(named, gate_weights[0][:, :, None], 0.0), axis=1).T
    live_pair = jnp.any(named, axis=1).T & slot_live[None, :]
    earlier = live_pair[:, :, None] & (order_of[:, :, None] < order_of[:, None, :])
    pair_rank = jnp.sum(earlier.astype(jnp.int32), axis=1)
    kept = live_pair & (pair_rank < capacity)
    place = jnp.where(kept, pair_rank.astype(F32), -1.0)
    meta = jnp.stack([place, jnp.where(kept, weight_of, 0.0)])
    meta = jnp.stack(gather_slots(meta, "ep"))
    meta = lax.dynamic_slice_in_dim(meta, my_ep * experts_dev, experts_dev, axis=2)
    place_in, weight_in = meta[:, 0], meta[:, 1]
    seats = jnp.arange(capacity, dtype=F32)
    chosen = place_in[:, :, None, :] == seats[None, None, :, None]
    row_weight = jnp.sum(jnp.where(chosen, weight_in[:, :, None, :], 0.0), axis=-1)
    row_weight = row_weight.reshape(n_ep, experts_dev * capacity, 1)
    pick = chosen.astype(LOW).reshape(n_ep, experts_dev * capacity, slot_count)

    scale_first = inv_rms(inputs)
    xn_own = (inputs * scale_first * gain_attn).astype(LOW)
    xn_first = jnp.stack(gather_slots(xn_own, "dp"))
    lens = jnp.stack(gather_slots(lengths, "dp"))
    projected = dot(xn_first.reshape(n_dp * slot_count, width), weight_qkv)
    projected = projected.reshape(n_dp, slot_count, 3, heads_dev, HEAD)
    query_raw, key_raw = projected[:, :, 0], projected[:, :, 1]
    values_low = projected[:, :, 2].astype(LOW)
    cosine, sine = rope_tables(slot_count, HEAD)
    query_scale, key_scale = inv_rms(query_raw), inv_rms(key_raw)
    query_rot = rotary(query_raw * query_scale * gain_query, cosine, sine).astype(LOW)
    key_rot = rotary(key_raw * key_scale * gain_key, cosine, sine).astype(LOW)
    raw = jnp.einsum("sqhd,skhd->shqk", query_rot, key_rot, preferred_element_type=F32) * factor
    key_live = slot_index[None, :] < lens
    scores = jnp.where(key_live[:, None, None, :], raw, NEG)
    probs = jax.nn.softmax(scores, axis=-1)
    probs_low = probs.astype(LOW)
    attended = jnp.einsum("shqk,skhd->sqhd", probs_low, values_low, preferred_element_type=F32)
    attended = attended.reshape(n_dp * slot_count, cols).astype(LOW)
    branch = dot(attended, weight_out).astype(LOW).reshape(n_dp, slot_count, width)
    resid = inputs + scatter_slots(list(branch), "dp")
    scale_second = inv_rms(resid)
    xn_second = (resid * scale_second * gain_ffn).astype(LOW)

    rows = jnp.einsum(
        "sct,std->scd", pick, jnp.stack(gather_slots(xn_second, "ep")), preferred_element_type=F32
    )
    received = rows.astype(LOW).reshape(n_ep, experts_dev, capacity, width)
    gate_up = jnp.einsum("sjcd,jdf->sjcf", received, expert_gate_up, preferred_element_type=F32)
    gate_part, up_part = gate_up[..., :hidden], gate_up[..., hidden:]
    sigmoid_gate = jax.nn.sigmoid(gate_part)
    activation = (gate_part * sigmoid_gate * up_part).astype(LOW)
    result = jnp.einsum("sjcf,jfd->sjcd", activation, expert_down, preferred_element_type=F32)
    result = result.reshape(n_ep, experts_dev * capacity, width) * row_weight
    mixed = jnp.einsum("sct,scd->std", pick, result.astype(LOW), preferred_element_type=F32)
    mixed = scatter_slots(list(mixed.astype(LOW)), "ep")
    output = (live_rows * (resid + mixed)).astype(LOW)

    grad_out = cotangent[0].astype(F32) * live_rows
    grad_rows = jnp.einsum(
        "sct,std->scd", pick, jnp.stack(gather_slots(cotangent[0], "ep")), preferred_element_type=F32
    )
    grad_recv = (grad_rows * row_weight).astype(LOW).reshape(n_ep, experts_dev, capacity, width)
    grad_act = jnp.einsum("sjcd,jfd->sjcf", grad_recv, expert_down, preferred_element_type=F32)
    grad_gate = grad_act * up_part * sigmoid_gate * (1.0 + gate_part * (1.0 - sigmoid_gate))
    grad_up = grad_act * gate_part * sigmoid_gate
    grad_gate_up = jnp.concatenate([grad_gate, grad_up], axis=-1).astype(LOW)
    back = jnp.einsum("sjcf,jdf->sjcd", grad_gate_up, expert_gate_up, preferred_element_type=F32)
    back = back.astype(LOW).reshape(n_ep, experts_dev * capacity, width)
    back = jnp.einsum("sct,scd->std", pick, back, preferred_element_type=F32)
    grad_xn_second = scatter_slots(list(back.astype(LOW)), "ep")
    grad_down = jnp.einsum("sjcf,sjcd->jfd", activation, grad_recv, preferred_element_type=F32)
    grad_weight_gu = jnp.einsum("sjcd,sjcf->jdf", received, grad_gate_up, preferred_element_type=F32)

    def expert_sum(grad):
        part = grad.shape[1] // n_dp
        parts = grad.astype(LOW).reshape(experts_dev, n_dp, part, width)
        return scatter_slots(
            [lax.dynamic_index_in_dim(parts, my_dp ^ r, axis=1, keepdims=False) for r in range(n_dp)], "dp"
        )

    down_grad = expert_sum(grad_down)
    gate_up_grad = expert_sum(grad_weight_gu)

    grad_resid = grad_out + norm_back(resid, scale_second, gain_ffn, grad_xn_second)
    grad_gain_ffn = jnp.sum(grad_xn_second * resid * scale_second, axis=0)
    grad_branch = jnp.stack(gather_slots(grad_resid.astype(LOW), "dp"))
    grad_branch = grad_branch.reshape(n_dp * slot_count, width)
    grad_wout = jnp.einsum("sa,sb->ab", attended, grad_branch, preferred_element_type=F32)
    grad_att = jnp.einsum("sb,ab->sa", grad_branch, weight_out, preferred_element_type=F32)
    grad_att = grad_att.astype(LOW).reshape(n_dp, slot_count, heads_dev, HEAD)
    grad_probs = jnp.einsum("sqhd,skhd->shqk", grad_att, values_low, preferred_element_type=F32)
    grad_values = jnp.einsum("shqk,sqhd->skhd", probs_low, grad_att, preferred_element_type=F32)
    inner_sum = jnp.sum(probs * grad_probs, axis=-1, keepdims=True)
    grad_scores = (probs * (grad_probs - inner_sum)).astype(LOW)
    grad_qrot = jnp.einsum("shqk,skhd->sqhd", grad_scores, key_rot, preferred_element_type=F32) * factor
    grad_krot = jnp.einsum("shqk,sqhd->skhd", grad_scores, query_rot, preferred_element_type=F32) * factor
    grad_qnorm = rotary(grad_qrot, cosine, -sine)
    grad_knorm = rotary(grad_krot, cosine, -sine)
    grad_query = norm_back(query_raw, query_scale, gain_query, grad_qnorm).astype(LOW)
    grad_key = norm_back(key_raw, key_scale, gain_key, grad_knorm).astype(LOW)
    grad_gain_query = jnp.sum(grad_qnorm * query_raw * query_scale, axis=(0, 1, 2))
    grad_gain_key = jnp.sum(grad_knorm * key_raw * key_scale, axis=(0, 1, 2))
    grad_proj = jnp.stack([grad_query, grad_key, grad_values.astype(LOW)], axis=2)
    grad_proj = grad_proj.reshape(n_dp * slot_count, 3 * cols)
    grad_wqkv = jnp.einsum(
        "sa,sb->ab",
        xn_first.reshape(n_dp * slot_count, width),
        grad_proj,
        preferred_element_type=F32,
    )
    grad_xn_first = jnp.einsum("sb,ab->sa", grad_proj, weight_qkv, preferred_element_type=F32)
    grad_xn_first = grad_xn_first.astype(LOW).reshape(n_dp, slot_count, width)
    grad_xn_first = scatter_slots(list(grad_xn_first), "dp")
    input_grad = grad_resid + norm_back(inputs, scale_first, gain_attn, grad_xn_first)
    grad_gain_attn = jnp.sum(grad_xn_first * inputs * scale_first, axis=0)

    parts = grad_wqkv.astype(LOW).reshape(n_dp, n_ep, rows_dev, 3 * cols)
    share = scatter_slots(
        [lax.dynamic_index_in_dim(parts, my_ep ^ s, axis=1, keepdims=False) for s in range(n_ep)], "ep"
    )
    qkv_share = jnp.zeros((rows_dev, 3, n_dp, cols), F32)
    for r in range(n_dp):
        piece = lax.dynamic_index_in_dim(share, my_dp ^ r, axis=0, keepdims=False)
        piece = swap(piece.astype(LOW), "dp", r).astype(F32) if r else piece
        piece = piece.reshape(rows_dev, 3, 1, cols)
        qkv_share = lax.dynamic_update_slice(qkv_share, piece, (0, 0, my_dp ^ r, 0))
    parts = grad_wout.astype(LOW).reshape(n_ep, rows_dev, width)
    out_share = scatter_slots(
        [lax.dynamic_index_in_dim(parts, my_ep ^ s, axis=0, keepdims=False) for s in range(n_ep)], "ep"
    )
    attn_share = jnp.concatenate([qkv_share.reshape(rows_dev, 3 * width), out_share], axis=1)

    gain_terms = jnp.concatenate([grad_gain_attn, grad_gain_ffn, grad_gain_query, grad_gain_key])
    gain_part = gain_terms.shape[0] // (n_dp * n_ep)
    gain_share = lax.dynamic_slice_in_dim(
        sum_all(gain_terms), (my_dp * n_ep + my_ep) * gain_part, gain_part
    )
    return (output[None], input_grad[None], attn_share, gain_share, gate_up_grad, down_grad)


def solution(mesh):
    in_specs = (
        P(("dp", "ep"), None, None),
        P(("dp", "ep")),
        P(("dp", "ep"), None, None),
        P(("dp", "ep"), None),
        P(("dp", "ep"), None, None),
        P(("dp", "ep"), None),
        P(),
        P("ep", None, None),
        P("ep", None, None),
        P(("dp", "ep"), None, None),
    )
    out_specs = (
        P(("dp", "ep"), None, None),
        P(("dp", "ep"), None, None),
        P(("dp", "ep"), None),
        P(("dp", "ep")),
        P("ep", "dp", None),
        P("ep", "dp", None),
    )
    return jax.shard_map(
        on_device, mesh=mesh, in_specs=in_specs, out_specs=out_specs, check_vma=False
    )
```

time: 2820 us -> 1180 us (0.42)
  waiting for transfers between devices: 2180 us -> 611 us
  starting transfers between devices: 20.8 us -> 73.4 us
  blocking collectives: 47.2 us -> 0 us
  other arithmetic: 128 us -> 98.8 us
    reduce_scatter x3 -> x0, waiting for transfers between devices: 1340 us -> none  [the longest x1 1340 us: on_device(): lax.psum_scatter(full_terms, ('dp', 'ep'), scatter_dimension=0, tiled=True)]
    all_to_all x4 -> x0, waiting for transfers between devices: 710 us -> none  [the longest x1 192 us: on_device(): lax.all_to_all(grad_rows.astype(jnp.bfloat16), 'ep', split_axis=0, concat...]
    ppermute x0 -> x95, waiting for transfers between devices: none -> 611 us  [swap(): return lax.ppermute(value, axis, [(i, i ^ mask) for i in range(count)])]
    all_gather x1 -> x0, waiting for transfers between devices: 135 us -> none  [on_device(): whole_weight = lax.all_gather(attn_weight, ('dp', 'ep'), axis=0, tiled=True)]
    gather x8 -> x0, local copies, waits for them, and re-layouts: 113 us -> none  [the longest x1 21.6 us: on_device(): rows_ext[dest_slot].astype(jnp.float32)]
    ppermute x0 -> x95, starting transfers between devices: none -> 73.4 us  [swap(): return lax.ppermute(value, axis, [(i, i ^ mask) for i in range(count)])]
    dynamic_update_slice x0 -> x24, local copies, waits for them, and re-layouts: none -> 49.6 us  [the longest x4 34.4 us: on_device(): qkv_share = lax.dynamic_update_slice(qkv_share, piece, (0, 0, my_dp ^ r, 0))]
    unnamed x1 -> x0, blocking collectives: 47.2 us -> none
  transfers between devices with their start and end apart: 8 -> 95, of which waited for: 6 -> 45; matrix products, arithmetic and copies ran while one was open for 16% -> 28% of each run, Pallas kernels for 0% -> 0%
where the time goes in v1:
time: 1180 us; the launch traced here: 1170 us
  waiting for transfers between devices  611 us (52%)
  matrix products  214 us (18%)
  local copies, waits for them, and re-layouts  171 us (14%)
  other arithmetic  98.8 us (8%)
  starting transfers between devices  73.4 us (6%)
    ppermute x95, waiting for transfers between devices, swap(): return lax.ppermute(value, axis, [(i, i ^ mask) for i in range(count)])  611 us
    ppermute x95, starting transfers between devices, swap(): return lax.ppermute(value, axis, [(i, i ^ mask) for i in range(count)])  73.4 us
    unnamed x153, local copies, waits for them, and re-layouts  36.2 us
    dynamic_update_slice x4, local copies, waits for them, and re-layouts, on_device(): qkv_share = lax.dynamic_update_slice(qkv_share, piece, (0, 0, my_dp ^ r, 0))  34.4 us
    dot_general x1, matrix products, on_device(): jnp.einsum('sjcd,sjcf->jdf', received, grad_gate_up, preferred_element_ty...  29.5 us
    dot_general x1, matrix products, on_device(): jnp.einsum('sjcd,jdf->sjcf', received, expert_gate_up, preferred_element_...  28.2 us
    convert_element_type x12, other arithmetic, scatter_slots(): acc[r] = acc[r] + swap(acc[r | bit].astype(LOW), axis, bit).astype(F32)  25.5 us
    dot_general x1, matrix products, on_device(): jnp.einsum('sjcf,jdf->sjcd', grad_gate_up, expert_gate_up, preferred_elem...  24.2 us
  transfers between devices with their start and end apart: 95, of which 45 were waited for; matrix products, arithmetic and copies ran while one was open for 28% of the time, Pallas kernels for 0%

profile of v1, /device:TPU:0, one launch (start us, length us, event | category | flops | bytes accessed | tf_op | source)
XLA Modules:
  0.0 1170.5 jit_solution(12779920002467827659)
XLA Ops:
  88.2 8.3 collective-permute-done.19
  98.4 13.8 %collective-permute-done.18 = bf16[64,2048]{1,0:T(8,128)(2,1)S(1)} collective-permute-done((bf16[64,2048]{1,0:T(8,128)(2,1)S(1)}, bf16[64,2048]{1,0:T(8,128)(2,1)S(1)}, u32[]{:S(2)}, u32[]{:S(2)}) %collective-permute-start.18) | collective-permute-done | bytes 262176 | tf_op jit(solution)/shard_map/ppermute | solution.py:18
  128.9 25.0 %collective-permute-done.7 = bf16[4,64,1536]{2,1,0:T(8,128)(2,1)S(1)} collective-permute-done((bf16[4,64,1536]{2,1,0:T(8,128)(2,1)S(1)}, bf16[4,64,1536]{2,1,0:T(8,128)(2,1)S(1)}, u32[]{:S(2)}, u32[]{:S(2)}) %collective-permute-start.7) | collective-permute-done | bytes 786464 | tf_op jit(solution)/shard_map/ppermute | solution.py:18
  156.4 16.3 %collective-permute-done.9 = bf16[4,64,1536]{2,1,0:T(8,128)(2,1)S(1)} collective-permute-done((bf16[4,64,1536]{2,1,0:T(8,128)(2,1)S(1)}, bf16[4,64,1536]{2,1,0:T(8,128)(2,1)S(1)}, u32[]{:S(2)}, u32[]{:S(2)}) %collective-permute-start.9) | collective-permute-done | bytes 786464 | tf_op jit(solution)/shard_map/ppermute | solution.py:18
  181.3 11.9 %collective-permute-done.10 = bf16[4,64,1536]{2,1,0:T(8,128)(2,1)S(1)} collective-permute-done((bf16[4,64,1536]{2,1,0:T(8,128)(2,1)S(1)}, bf16[4,64,1536]{2,1,0:T(8,128)(2,1)S(1)}, u32[]{:S(2)}, u32[]{:S(2)}) %collective-permute-start.10) | collective-permute-done | bytes 786464 | tf_op jit(solution)/shard_map/ppermute | solution.py:18
  197.0 32.8 %collective-permute-done.12 = bf16[4,64,1536]{2,1,0:T(8,128)(2,1)S(1)} collective-permute-done((bf16[4,64,1536]{2,1,0:T(8,128)(2,1)S(1)}, bf16[4,64,1536]{2,1,0:T(8,128)(2,1)S(1)}, u32[]{:S(2)}, u32[]{:S(2)}) %collective-permute-start.12) | collective-permute-done | bytes 786464 | tf_op jit(solution)/shard_map/ppermute | solution.py:18
  235.4 8.6 copy.219
  244.6 10.6 fusion.36
  276.6 12.8 %collective-permute-done.50 = bf16[256,2048]{1,0:T(8,128)(2,1)} collective-permute-done((bf16[256,2048]{1,0:T(8,128)(2,1)S(1)}, bf16[256,2048]{1,0:T(8,128)(2,1)}, u32[]{:S(2)}, u32[]{:S(2)}) %collective-permute-start.50) | collective-permute-done | bytes 1048608 | tf_op jit(solution)/shard_map/ppermute | solution.py:18
  300.2 14.8 %collective-permute-done.52 = bf16[256,2048]{1,0:T(8,128)(2,1)S(1)} collective-permute-done((bf16[256,2048]{1,0:T(8,128)(2,1)}, bf16[256,2048]{1,0:T(8,128)(2,1)S(1)}, u32[]{:S(2)}, u32[]{:S(2)}) %collective-permute-start.52) | collective-permute-done | bytes 1048608 | tf_op jit(solution)/shard_map/ppermute | solution.py:18
  316.4 21.7 %collective-permute-done.49 = bf16[256,2048]{1,0:T(8,128)(2,1)S(1)} collective-permute-done((bf16[256,2048]{1,0:T(8,128)(2,1)}, bf16[256,2048]{1,0:T(8,128)(2,1)S(1)}, u32[]{:S(2)}, u32[]{:S(2)}) %collective-permute-start.49) | collective-permute-done | bytes 1048608 | tf_op jit(solution)/shard_map/ppermute | solution.py:18
  347.2 13.3 %collective-permute-done.53 = bf16[256,2048]{1,0:T(8,128)(2,1)S(1)} collective-permute-done((bf16[256,2048]{1,0:T(8,128)(2,1)S(1)}, bf16[256,2048]{1,0:T(8,128)(2,1)S(1)}, u32[]{:S(2)}, u32[]{:S(2)}) %collective-permute-start.53) | collective-permute-done | bytes 1048608 | tf_op jit(solution)/shard_map/ppermute | solution.py:18
  360.6 28.6 %collective-permute-done.34 = bf16[256,2048]{1,0:T(8,128)(2,1)S(1)} collective-permute-done((bf16[256,2048]{1,0:T(8,128)(2,1)S(1)}, bf16[256,2048]{1,0:T(8,128)(2,1)S(1)}, u32[]{:S(2)}, u32[]{:S(2)}) %collective-permute-start.34) | collective-permute-done | bytes 1048608 | tf_op jit(solution)/shard_map/ppermute | solution.py:18
  401.2 13.5 %collective-permute-done.38 = bf16[256,2048]{1,0:T(8,128)(2,1)} collective-permute-done((bf16[256,2048]{1,0:T(8,128)(2,1)S(1)}, bf16[256,2048]{1,0:T(8,128)(2,1)}, u32[]{:S(2)}, u32[]{:S(2)}) %collective-permute-start.38) | collective-permute-done | bytes 1048608 | tf_op jit(solution)/shard_map/ppermute | solution.py:18
  418.8 19.0 %collective-permute-done.37 = bf16[256,2048]{1,0:T(8,128)(2,1)S(1)} collective-permute-done((bf16[256,2048]{1,0:T(8,128)(2,1)S(1)}, bf16[256,2048]{1,0:T(8,128)(2,1)S(1)}, u32[]{:S(2)}, u32[]{:S(2)}) %collective-permute-start.37) | collective-permute-done | bytes 1048608 | tf_op jit(solution)/shard_map/ppermute | solution.py:18
  441.1 17.1 %collective-permute-done.39 = bf16[256,2048]{1,0:T(8,128)(2,1)S(1)} collective-permute-done((bf16[256,2048]{1,0:T(8,128)(2,1)}, bf16[256,2048]{1,0:T(8,128)(2,1)S(1)}, u32[]{:S(2)}, u32[]{:S(2)}) %collective-permute-start.39) | collective-permute-done | bytes 1048608 | tf_op jit(solution)/shard_map/ppermute | solution.py:18
  465.3 28.2 %fusion.25 = f32[8,2,144,2048]{3,2,0,1:T(8,128)} fusion(bf16[2,2048,2048]{2,1,0:T(8,128)(2,1)} %param.17, bf16[8,2,144,2048]{3,2,1,0:T(8,128)(2,1)S(1)} %bitcast.495), kind=kOutput, calls=%fused_computation.36 | convolution fusion | flops 19327352832 | bytes 45088768 | tf_op jit(solution)/shard_map/sjcd,jdf->sjcf/dot_general | solution.py:181
  493.5 22.8 %fusion.8 = (bf16[8,2,144,1024]{3,2,0,1:T(8,128)(2,1)}, bf16[8,2,144,1024]{3,2,0,1:T(8,128)(2,1)}, bf16[8,2,144,1024]{3,2,0,1:T(8,128)(2,1)}) fusion(f32[8,2,144,2048]{3,2,0,1:T(8,128)} %fusion.25, bf16[2,1024,2048]{2,1,0:T(8,128)(2,1)} %param.18, bf16[8,2,144,2048]{3,2,1,0:T(8,128)(2,1)} %bitcast.500), kind=kOutput, calls=%fused_computation.15 | convolution fusion | flops 9701425152 | bytes 50855936 | tf_op jit(solution)/shard_map/sjcd,jfd->sjcf/dot_general | solution.py:196
  516.4 17.9 %fusion.22 = f32[8,2,144,2048]{3,2,0,1:T(8,128)} fusion(bf16[8,2,144,1024]{3,2,0,1:T(8,128)(2,1)} %get-tuple-element.30, bf16[2,1024,2048]{2,1,0:T(8,128)(2,1)} %param.18), kind=kOutput, calls=%fused_computation.35 | convolution fusion | flops 9663676416 | bytes 31981568 | tf_op jit(solution)/shard_map/sjcf,jfd->sjcd/dot_general | solution.py:185
  546.2 24.2 %convert_bitcast_fusion = bf16[8,2,144,2048]{3,2,0,1:T(8,128)(2,1)} fusion(bf16[2,2048,2048]{2,1,0:T(8,128)(2,1)} %param.17, bf16[8,2,144,1024]{3,2,0,1:T(8,128)(2,1)S(1)} %bitcast.545, bf16[8,2,144,1024]{3,2,0,1:T(8,128)(2,1)S(1)} %bitcast.543), kind=kOutput, calls=%fused_computation.20 | convolution fusion | flops 19350945792 | bytes 35651584 | tf_op jit(solution)/shard_map/sjcf,jdf->sjcd/dot_general | solution.py:200
  570.4 9.2 copy.184
  579.6 8.5 convolution_convert_fusion.2
  591.8 10.6 convolution_convert_fusion.3
  615.9 22.5 %collective-permute-done.58 = bf16[256,2048]{1,0:T(8,128)(2,1)S(1)} collective-permute-done((bf16[256,2048]{1,0:T(8,128)(2,1)S(1)}, bf16[256,2048]{1,0:T(8,128)(2,1)S(1)}, u32[]{:S(2)}, u32[]{:S(2)}) %collective-permute-start.58) | collective-permute-done | bytes 1048608 | tf_op jit(solution)/shard_map/ppermute | solution.py:18
  640.8 20.1 %collective-permute-done.41 = bf16[256,2048]{1,0:T(8,128)(2,1)S(1)} collective-permute-done((bf16[256,2048]{1,0:T(8,128)(2,1)S(1)}, bf16[256,2048]{1,0:T(8,128)(2,1)S(1)}, u32[]{:S(2)}, u32[]{:S(2)}) %collective-permute-start.41) | collective-permute-done | bytes 1048608 | tf_op jit(solution)/shard_map/ppermute | solution.py:18
  660.8 22.5 %collective-permute-done.44 = bf16[256,2048]{1,0:T(8,128)(2,1)S(1)} collective-permute-done((bf16[256,2048]{1,0:T(8,128)(2,1)S(1)}, bf16[256,2048]{1,0:T(8,128)(2,1)S(1)}, u32[]{:S(2)}, u32[]{:S(2)}) %collective-permute-start.44) | collective-permute-done | bytes 1048608 | tf_op jit(solution)/shard_map/ppermute | solution.py:18
  687.6 18.2 %collective-permute-done.57 = bf16[256,2048]{1,0:T(8,128)(2,1)S(1)} collective-permute-done((bf16[256,2048]{1,0:T(8,128)(2,1)S(1)}, bf16[256,2048]{1,0:T(8,128)(2,1)S(1)}, u32[]{:S(2)}, u32[]{:S(2)}) %collective-permute-start.57) | collective-permute-done | bytes 1048608 | tf_op jit(solution)/shard_map/ppermute | solution.py:18
  707.3 21.1 %collective-permute-done.43 = bf16[256,2048]{1,0:T(8,128)(2,1)} collective-permute-done((bf16[256,2048]{1,0:T(8,128)(2,1)}, bf16[256,2048]{1,0:T(8,128)(2,1)}, u32[]{:S(2)}, u32[]{:S(2)}) %collective-permute-start.43) | collective-permute-done | bytes 1048608 | tf_op jit(solution)/shard_map/ppermute | solution.py:18
  731.5 19.2 %collective-permute-done.54 = bf16[256,2048]{1,0:T(8,128)(2,1)S(1)} collective-permute-done((bf16[256,2048]{1,0:T(8,128)(2,1)}, bf16[256,2048]{1,0:T(8,128)(2,1)S(1)}, u32[]{:S(2)}, u32[]{:S(2)}) %collective-permute-start.54) | collective-permute-done | bytes 1048608 | tf_op jit(solution)/shard_map/ppermute | solution.py:18
  754.3 13.6 %collective-permute-done.56 = bf16[256,2048]{1,0:T(8,128)(2,1)S(1)} collective-permute-done((bf16[256,2048]{1,0:T(8,128)(2,1)}, bf16[256,2048]{1,0:T(8,128)(2,1)S(1)}, u32[]{:S(2)}, u32[]{:S(2)}) %collective-permute-start.56) | collective-permute-done | bytes 1048608 | tf_op jit(solution)/shard_map/ppermute | solution.py:18
  770.8 25.6 %collective-permute-done.42 = bf16[256,2048]{1,0:T(8,128)(2,1)S(1)} collective-permute-done((bf16[256,2048]{1,0:T(8,128)(2,1)}, bf16[256,2048]{1,0:T(8,128)(2,1)S(1)}, u32[]{:S(2)}, u32[]{:S(2)}) %collective-permute-start.42) | collective-permute-done | bytes 1048608 | tf_op jit(solution)/shard_map/ppermute | solution.py:18
  803.1 29.5 %bitcast_convert_fusion = bf16[2,2048,2048]{2,1,0:T(8,128)(2,1)} fusion(bf16[8,2,144,2048]{3,2,1,0:T(8,128)(2,1)} %bitcast.496, bf16[8,2,144,1024]{3,2,0,1:T(8,128)(2,1)} %get-tuple-element.29, bf16[8,2,144,1024]{3,2,0,1:T(8,128)(2,1)} %get-tuple-element.28), kind=kOutput, calls=%fused_computation.1 | convolution fusion | flops 19354615808 | bytes 35651584 | tf_op jit(solution)/shard_map/sjcd,sjcf->jdf/dot_general | solution.py:205
  833.1 15.3 %bitcast_convert_fusion.1 = bf16[2,1024,2048]{2,1,0:T(8,128)(2,1)S(1)} fusion(bf16[8,2,144,1024]{3,2,0,1:T(8,128)(2,1)} %get-tuple-element.30, bf16[8,2,144,2048]{3,2,1,0:T(8,128)(2,1)} %bitcast.501), kind=kOutput, calls=%fused_computation.5 | convolution fusion | flops 9667870720 | bytes 22544384 | tf_op jit(solution)/shard_map/sjcf,sjcd->jfd/dot_general | solution.py:204
  853.6 8.4 dynamic-slice_bitcast_fusion.1
  892.8 8.8 convolution_convert_fusion.4
  910.4 7.8 convolution_convert_fusion
  919.4 15.8 %collective-permute-done.66 = bf16[256,2048]{1,0:T(8,128)(2,1)S(1)} collective-permute-done((bf16[256,2048]{1,0:T(8,128)(2,1)S(1)}, bf16[256,2048]{1,0:T(8,128)(2,1)S(1)}, u32[]{:S(2)}, u32[]{:S(2)}) %collective-permute-start.66) | collective-permute-done | bytes 1048608 | tf_op jit(solution)/shard_map/ppermute | solution.py:18
  954.6 10.4 collective-permute-done.80
  973.0 13.9 %collective-permute-done.94 = bf16[2,256,2048]{2,1,0:T(8,128)(2,1)S(1)} collective-permute-done((bf16[2,256,2048]{2,1,0:T(8,128)(2,1)S(1)}, bf16[2,256,2048]{2,1,0:T(8,128)(2,1)S(1)}, u32[]{:S(2)}, u32[]{:S(2)}) %collective-permute-start.94) | collective-permute-done | bytes 2097184 | tf_op jit(solution)/shard_map/ppermute | solution.py:18
  995.8 12.2 %collective-permute-done.68 = bf16[4,64,1536]{2,1,0:T(8,128)(2,1)S(1)} collective-permute-done((bf16[4,64,1536]{2,1,0:T(8,128)(2,1)}, bf16[4,64,1536]{2,1,0:T(8,128)(2,1)S(1)}, u32[]{:S(2)}, u32[]{:S(2)}) %collective-permute-start.68) | collective-permute-done | bytes 786464 | tf_op jit(solution)/shard_map/ppermute | solution.py:18
  1009.5 15.4 %collective-permute-done.70 = bf16[4,64,1536]{2,1,0:T(8,128)(2,1)S(1)} collective-permute-done((bf16[4,64,1536]{2,1,0:T(8,128)(2,1)S(1)}, bf16[4,64,1536]{2,1,0:T(8,128)(2,1)S(1)}, u32[]{:S(2)}, u32[]{:S(2)}) %collective-permute-start.70) | collective-permute-done | bytes 786464 | tf_op jit(solution)/shard_map/ppermute | solution.py:18
  1026.9 53.5 %collective-permute-done.88 = f32[4352]{0:T(1024)S(1)} collective-permute-done((f32[4352]{0:T(1024)S(1)}, f32[4352]{0:T(1024)S(1)}, u32[]{:S(2)}, u32[]{:S(2)}) %collective-permute-start.88) | collective-permute-done | bytes 17440 | tf_op jit(solution)/shard_map/ppermute | solution.py:18
  1084.5 32.1 %collective-permute-done.73 = bf16[4,64,1536]{2,1,0:T(8,128)(2,1)S(1)} collective-permute-done((bf16[4,64,1536]{2,1,0:T(8,128)(2,1)S(1)}, bf16[4,64,1536]{2,1,0:T(8,128)(2,1)S(1)}, u32[]{:S(2)}, u32[]{:S(2)}) %collective-permute-start.73) | collective-permute-done | bytes 786464 | tf_op jit(solution)/shard_map/ppermute | solution.py:18
  1119.7 8.6 dynamic_update_slice.92
  1128.8 8.6 dynamic_update_slice.93
  1137.9 8.7 dynamic_update_slice.94
  1147.2 8.6 dynamic_update_slice.95
  1159.4 11.0 fusion.14
  (455 shorter events, 347.3 us)
Async XLA Ops:
  6.1 173.7 %collective-permute-start.1 = (bf16[256,2048]{1,0:T(8,128)(2,1)}, bf16[256,2048]{1,0:T(8,128)(2,1)}, u32[]{:S(2)}, u32[]{:S(2)}) collective-permute-start(bf16[256,2048]{1,0:T(8,128)(2,1)} %fusion.47), channel_id=1, source_target_pairs={{0,16},{8,24},{16,0},{24,8},{1,17},{9,25},{17,1},{25,9},{2,18},{10... | collective-permute-start | bytes 3145736 | tf_op jit(solution)/shard_map/ppermute | solution.py:18
  9.0 235.0 %collective-permute-start = (bf16[256,2048]{1,0:T(8,128)(2,1)}, bf16[256,2048]{1,0:T(8,128)(2,1)}, u32[]{:S(2)}, u32[]{:S(2)}) collective-permute-start(bf16[256,2048]{1,0:T(8,128)(2,1)} %fusion.47), channel_id=1, source_target_pairs={{0,8},{8,0},{16,24},{24,16},{1,9},{9,1},{17,25},{25,17},{2,10},{10... | collective-permute-start | bytes 3145736 | tf_op jit(solution)/shard_map/ppermute | solution.py:18
  9.0 36.2 %collective-permute-start.14 = (s32[1]{0:T(128)}, s32[1]{0:T(128)}, u32[]{:S(2)}, u32[]{:S(2)}) collective-permute-start(s32[1]{0:T(128)} %param.11), channel_id=1, source_target_pairs={{0,16},{8,24},{16,0},{24,8},{1,17},{9,25},{17,1},{25,9},{2,18},{10... | collective-permute-start | bytes 20 | tf_op jit(solution)/shard_map/ppermute | solution.py:18
  9.1 37.8 %collective-permute-start.13 = (s32[1]{0:T(128)}, s32[1]{0:T(128)}, u32[]{:S(2)}, u32[]{:S(2)}) collective-permute-start(s32[1]{0:T(128)} %param.11), channel_id=1, source_target_pairs={{0,8},{8,0},{16,24},{24,16},{1,9},{9,1},{17,25},{25,17},{2,10},{10... | collective-permute-start | bytes 20 | tf_op jit(solution)/shard_map/ppermute | solution.py:18
  16.5 36.3 %collective-permute-start.26 = (f32[2,16,256]{2,1,0:T(8,128)}, f32[2,16,256]{2,1,0:T(8,128)}, u32[]{:S(2)}, u32[]{:S(2)}) collective-permute-start(f32[2,16,256]{2,1,0:T(8,128)} %pad_maximum_fusion.13), channel_id=1, source_target_pairs={{0,1},{1,0},{2,3},{3,2},{4,5},{5,4},{6,7},{7,6},{8,9},{9,8},{10,11... | collective-permute-start | bytes 98312 | tf_op jit(solution)/shard_map/ppermute | solution.py:18
  86.1 40.2 %collective-permute-start.6 = (bf16[4,64,1536]{2,1,0:T(8,128)(2,1)S(1)}, bf16[4,64,1536]{2,1,0:T(8,128)(2,1)S(1)}, u32[]{:S(2)}, u32[]{:S(2)}) collective-permute-start(bf16[4,64,1536]{2,1,0:T(8,128)(2,1)S(1)} %bitcast_dynamic-update-slice_fusion.31), channel_id=1, source_target_pairs={{0,1},{1,0},{2,3},{3,2},{4,5},{5,4},{6,7},{7,6},{8,9},{9,8},{10,11... | collective-permute-start | bytes 2359304 | tf_op jit(solution)/shard_map/ppermute | solution.py:18
  116.7 37.3 %collective-permute-start.7 = (bf16[4,64,1536]{2,1,0:T(8,128)(2,1)S(1)}, bf16[4,64,1536]{2,1,0:T(8,128)(2,1)S(1)}, u32[]{:S(2)}, u32[]{:S(2)}) collective-permute-start(bf16[4,64,1536]{2,1,0:T(8,128)(2,1)S(1)} %bitcast_dynamic-update-slice_fusion.31), channel_id=1, source_target_pairs={{0,2},{1,3},{2,0},{3,1},{4,6},{5,7},{6,4},{7,5},{8,10},{9,11},{10,... | collective-permute-start | bytes 2359304 | tf_op jit(solution)/shard_map/ppermute | solution.py:18
  125.2 164.8 %collective-permute-start.48 = (bf16[256,2048]{1,0:T(8,128)(2,1)S(1)}, bf16[256,2048]{1,0:T(8,128)(2,1)}, u32[]{:S(2)}, u32[]{:S(2)}) collective-permute-start(bf16[256,2048]{1,0:T(8,128)(2,1)S(1)} %bitcast.517), channel_id=1, source_target_pairs={{0,2},{1,3},{2,0},{3,1},{4,6},{5,7},{6,4},{7,5},{8,10},{9,11},{10,... | collective-permute-start | bytes 3145736 | tf_op jit(solution)/shard_map/ppermute | solution.py:18
  126.3 46.3 %collective-permute-start.9 = (bf16[4,64,1536]{2,1,0:T(8,128)(2,1)S(1)}, bf16[4,64,1536]{2,1,0:T(8,128)(2,1)S(1)}, u32[]{:S(2)}, u32[]{:S(2)}) collective-permute-start(bf16[4,64,1536]{2,1,0:T(8,128)(2,1)S(1)} %bitcast_dynamic-update-slice_fusion.31), channel_id=1, source_target_pairs={{0,4},{1,5},{2,6},{3,7},{4,0},{5,1},{6,2},{7,3},{8,12},{9,13},{10,... | collective-permute-start | bytes 2359304 | tf_op jit(solution)/shard_map/ppermute | solution.py:18
  179.7 111.7 %collective-permute-start.47 = (bf16[256,2048]{1,0:T(8,128)(2,1)S(1)}, bf16[256,2048]{1,0:T(8,128)(2,1)}, u32[]{:S(2)}, u32[]{:S(2)}) collective-permute-start(bf16[256,2048]{1,0:T(8,128)(2,1)S(1)} %bitcast.518), channel_id=1, source_target_pairs={{0,1},{1,0},{2,3},{3,2},{4,5},{5,4},{6,7},{7,6},{8,9},{9,8},{10,11... | collective-permute-start | bytes 3145736 | tf_op jit(solution)/shard_map/ppermute | solution.py:18
  193.2 51.5 %collective-permute-start.2 = (bf16[256,2048]{1,0:T(8,128)(2,1)}, bf16[256,2048]{1,0:T(8,128)(2,1)}, u32[]{:S(2)}, u32[]{:S(2)}) collective-permute-start(bf16[256,2048]{1,0:T(8,128)(2,1)} %collective-permute-done.1), channel_id=1, source_target_pairs={{0,8},{8,0},{16,24},{24,16},{1,9},{9,1},{17,25},{25,17},{2,10},{10... | collective-permute-start | bytes 3145736 | tf_op jit(solution)/shard_map/ppermute | solution.py:18
  193.6 36.2 %collective-permute-start.12 = (bf16[4,64,1536]{2,1,0:T(8,128)(2,1)S(1)}, bf16[4,64,1536]{2,1,0:T(8,128)(2,1)S(1)}, u32[]{:S(2)}, u32[]{:S(2)}) collective-permute-start(bf16[4,64,1536]{2,1,0:T(8,128)(2,1)S(1)} %collective-permute-done.11), channel_id=1, source_target_pairs={{0,1},{1,0},{2,3},{3,2},{4,5},{5,4},{6,7},{7,6},{8,9},{9,8},{10,11... | collective-permute-start | bytes 2359304 | tf_op jit(solution)/shard_map/ppermute | solution.py:18
  244.0 45.3 %collective-permute-start.50 = (bf16[256,2048]{1,0:T(8,128)(2,1)S(1)}, bf16[256,2048]{1,0:T(8,128)(2,1)}, u32[]{:S(2)}, u32[]{:S(2)}) collective-permute-start(bf16[256,2048]{1,0:T(8,128)(2,1)S(1)} %bitcast.519), channel_id=1, source_target_pairs={{0,4},{1,5},{2,6},{3,7},{4,0},{5,1},{6,2},{7,3},{8,12},{9,13},{10,... | collective-permute-start | bytes 3145736 | tf_op jit(solution)/shard_map/ppermute | solution.py:18
  289.3 57.3 %collective-permute-start.51 = (bf16[256,2048]{1,0:T(8,128)(2,1)}, bf16[256,2048]{1,0:T(8,128)(2,1)S(1)}, u32[]{:S(2)}, u32[]{:S(2)}) collective-permute-start(bf16[256,2048]{1,0:T(8,128)(2,1)} %collective-permute-done.50), channel_id=1, source_target_pairs={{0,1},{1,0},{2,3},{3,2},{4,5},{5,4},{6,7},{7,6},{8,9},{9,8},{10,11... | collective-permute-start | bytes 3145736 | tf_op jit(solution)/shard_map/ppermute | solution.py:18
  290.0 48.1 %collective-permute-start.49 = (bf16[256,2048]{1,0:T(8,128)(2,1)}, bf16[256,2048]{1,0:T(8,128)(2,1)S(1)}, u32[]{:S(2)}, u32[]{:S(2)}) collective-permute-start(bf16[256,2048]{1,0:T(8,128)(2,1)} %collective-permute-done.48), channel_id=1, source_target_pairs={{0,1},{1,0},{2,3},{3,2},{4,5},{5,4},{6,7},{7,6},{8,9},{9,8},{10,11... | collective-permute-start | bytes 3145736 | tf_op jit(solution)/shard_map/ppermute | solution.py:18
  293.7 47.8 %collective-permute-start.23 = (bf16[256,2048]{1,0:T(8,128)(2,1)}, bf16[256,2048]{1,0:T(8,128)(2,1)S(1)}, u32[]{:S(2)}, u32[]{:S(2)}) collective-permute-start(bf16[256,2048]{1,0:T(8,128)(2,1)} %get-tuple-element.59), channel_id=1, source_target_pairs={{0,8},{8,0},{16,24},{24,16},{1,9},{9,1},{17,25},{25,17},{2,10},{10... | collective-permute-start | bytes 3145736 | tf_op jit(solution)/shard_map/ppermute | solution.py:18
  295.7 45.8 %collective-permute-start.25 = (bf16[256,2048]{1,0:T(8,128)(2,1)S(1)}, bf16[256,2048]{1,0:T(8,128)(2,1)S(1)}, u32[]{:S(2)}, u32[]{:S(2)}) collective-permute-start(bf16[256,2048]{1,0:T(8,128)(2,1)S(1)} %add_convert_fusion.1), channel_id=1, source_target_pairs={{0,16},{8,24},{16,0},{24,8},{1,17},{9,25},{17,1},{25,9},{2,18},{10... | collective-permute-start | bytes 3145736 | tf_op jit(solution)/shard_map/ppermute | solution.py:18
  315.0 45.6 %collective-permute-start.53 = (bf16[256,2048]{1,0:T(8,128)(2,1)S(1)}, bf16[256,2048]{1,0:T(8,128)(2,1)S(1)}, u32[]{:S(2)}, u32[]{:S(2)}) collective-permute-start(bf16[256,2048]{1,0:T(8,128)(2,1)S(1)} %collective-permute-done.52), channel_id=1, source_target_pairs={{0,1},{1,0},{2,3},{3,2},{4,5},{5,4},{6,7},{7,6},{8,9},{9,8},{10,11... | collective-permute-start | bytes 3145736 | tf_op jit(solution)/shard_map/ppermute | solution.py:18
  345.4 43.8 %collective-permute-start.34 = (bf16[256,2048]{1,0:T(8,128)(2,1)S(1)}, bf16[256,2048]{1,0:T(8,128)(2,1)S(1)}, u32[]{:S(2)}, u32[]{:S(2)}) collective-permute-start(bf16[256,2048]{1,0:T(8,128)(2,1)S(1)} %get-tuple-element.25), channel_id=1, source_target_pairs={{0,2},{1,3},{2,0},{3,1},{4,6},{5,7},{6,4},{7,5},{8,10},{9,11},{10,... | collective-permute-start | bytes 3145736 | tf_op jit(solution)/shard_map/ppermute | solution.py:18
  345.4 46.8 %collective-permute-start.36 = (bf16[256,2048]{1,0:T(8,128)(2,1)S(1)}, bf16[256,2048]{1,0:T(8,128)(2,1)S(1)}, u32[]{:S(2)}, u32[]{:S(2)}) collective-permute-start(bf16[256,2048]{1,0:T(8,128)(2,1)S(1)} %get-tuple-element.25), channel_id=1, source_target_pairs={{0,4},{1,5},{2,6},{3,7},{4,0},{5,1},{6,2},{7,3},{8,12},{9,13},{10,... | collective-permute-start | bytes 3145736 | tf_op jit(solution)/shard_map/ppermute | solution.py:18
  346.8 51.0 %collective-permute-start.33 = (bf16[256,2048]{1,0:T(8,128)(2,1)S(1)}, bf16[256,2048]{1,0:T(8,128)(2,1)}, u32[]{:S(2)}, u32[]{:S(2)}) collective-permute-start(bf16[256,2048]{1,0:T(8,128)(2,1)S(1)} %get-tuple-element.25), channel_id=1, source_target_pairs={{0,1},{1,0},{2,3},{3,2},{4,5},{5,4},{6,7},{7,6},{8,9},{9,8},{10,11... | collective-permute-start | bytes 3145736 | tf_op jit(solution)/shard_map/ppermute | solution.py:18
  397.2 40.5 %collective-permute-start.37 = (bf16[256,2048]{1,0:T(8,128)(2,1)S(1)}, bf16[256,2048]{1,0:T(8,128)(2,1)S(1)}, u32[]{:S(2)}, u32[]{:S(2)}) collective-permute-start(bf16[256,2048]{1,0:T(8,128)(2,1)S(1)} %collective-permute-done.36), channel_id=1, source_target_pairs={{0,1},{1,0},{2,3},{3,2},{4,5},{5,4},{6,7},{7,6},{8,9},{9,8},{10,11... | collective-permute-start | bytes 3145736 | tf_op jit(solution)/shard_map/ppermute | solution.py:18
  414.7 43.6 %collective-permute-start.39 = (bf16[256,2048]{1,0:T(8,128)(2,1)}, bf16[256,2048]{1,0:T(8,128)(2,1)S(1)}, u32[]{:S(2)}, u32[]{:S(2)}) collective-permute-start(bf16[256,2048]{1,0:T(8,128)(2,1)} %collective-permute-done.38), channel_id=1, source_target_pairs={{0,1},{1,0},{2,3},{3,2},{4,5},{5,4},{6,7},{7,6},{8,9},{9,8},{10,11... | collective-permute-start | bytes 3145736 | tf_op jit(solution)/shard_map/ppermute | solution.py:18
  590.4 47.9 %collective-permute-start.58 = (bf16[256,2048]{1,0:T(8,128)(2,1)S(1)}, bf16[256,2048]{1,0:T(8,128)(2,1)S(1)}, u32[]{:S(2)}, u32[]{:S(2)}) collective-permute-start(bf16[256,2048]{1,0:T(8,128)(2,1)S(1)} %get-tuple-element.36), channel_id=1, source_target_pairs={{0,1},{1,0},{2,3},{3,2},{4,5},{5,4},{6,7},{7,6},{8,9},{9,8},{10,11... | collective-permute-start | bytes 3145736 | tf_op jit(solution)/shard_map/ppermute | solution.py:18
  606.5 54.4 %collective-permute-start.41 = (bf16[256,2048]{1,0:T(8,128)(2,1)S(1)}, bf16[256,2048]{1,0:T(8,128)(2,1)S(1)}, u32[]{:S(2)}, u32[]{:S(2)}) collective-permute-start(bf16[256,2048]{1,0:T(8,128)(2,1)S(1)} %get-tuple-element.44), channel_id=1, source_target_pairs={{0,1},{1,0},{2,3},{3,2},{4,5},{5,4},{6,7},{7,6},{8,9},{9,8},{10,11... | collective-permute-start | bytes 3145736 | tf_op jit(solution)/shard_map/ppermute | solution.py:18
  607.1 76.2 %collective-permute-start.44 = (bf16[256,2048]{1,0:T(8,128)(2,1)S(1)}, bf16[256,2048]{1,0:T(8,128)(2,1)S(1)}, u32[]{:S(2)}, u32[]{:S(2)}) collective-permute-start(bf16[256,2048]{1,0:T(8,128)(2,1)S(1)} %get-tuple-element.42), channel_id=1, source_target_pairs={{0,1},{1,0},{2,3},{3,2},{4,5},{5,4},{6,7},{7,6},{8,9},{9,8},{10,11... | collective-permute-start | bytes 3145736 | tf_op jit(solution)/shard_map/ppermute | solution.py:18
  608.5 97.3 %collective-permute-start.57 = (bf16[256,2048]{1,0:T(8,128)(2,1)S(1)}, bf16[256,2048]{1,0:T(8,128)(2,1)S(1)}, u32[]{:S(2)}, u32[]{:S(2)}) collective-permute-start(bf16[256,2048]{1,0:T(8,128)(2,1)S(1)} %get-tuple-element.37), channel_id=1, source_target_pairs={{0,1},{1,0},{2,3},{3,2},{4,5},{5,4},{6,7},{7,6},{8,9},{9,8},{10,11... | collective-permute-start | bytes 3145736 | tf_op jit(solution)/shard_map/ppermute | solution.py:18
  640.1 65.6 %collective-permute-start.59 = (bf16[256,2048]{1,0:T(8,128)(2,1)S(1)}, bf16[256,2048]{1,0:T(8,128)(2,1)S(1)}, u32[]{:S(2)}, u32[]{:S(2)}) collective-permute-start(bf16[256,2048]{1,0:T(8,128)(2,1)S(1)} %get-tuple-element.40), channel_id=1, source_target_pairs={{0,2},{1,3},{2,0},{3,1},{4,6},{5,7},{6,4},{7,5},{8,10},{9,11},{10,... | collective-permute-start | bytes 3145736 | tf_op jit(solution)/shard_map/ppermute | solution.py:18
  640.2 88.2 %collective-permute-start.43 = (bf16[256,2048]{1,0:T(8,128)(2,1)}, bf16[256,2048]{1,0:T(8,128)(2,1)}, u32[]{:S(2)}, u32[]{:S(2)}) collective-permute-start(bf16[256,2048]{1,0:T(8,128)(2,1)} %get-tuple-element.43), channel_id=1, source_target_pairs={{0,1},{1,0},{2,3},{3,2},{4,5},{5,4},{6,7},{7,6},{8,9},{9,8},{10,11... | collective-permute-start | bytes 3145736 | tf_op jit(solution)/shard_map/ppermute | solution.py:18
  687.0 42.0 %collective-permute-start.45 = (bf16[256,2048]{1,0:T(8,128)(2,1)}, bf16[256,2048]{1,0:T(8,128)(2,1)}, u32[]{:S(2)}, u32[]{:S(2)}) collective-permute-start(bf16[256,2048]{1,0:T(8,128)(2,1)} %get-tuple-element.46), channel_id=1, source_target_pairs={{0,2},{1,3},{2,0},{3,1},{4,6},{5,7},{6,4},{7,5},{8,10},{9,11},{10,... | collective-permute-start | bytes 3145736 | tf_op jit(solution)/shard_map/ppermute | solution.py:18
  687.0 63.8 %collective-permute-start.54 = (bf16[256,2048]{1,0:T(8,128)(2,1)}, bf16[256,2048]{1,0:T(8,128)(2,1)S(1)}, u32[]{:S(2)}, u32[]{:S(2)}) collective-permute-start(bf16[256,2048]{1,0:T(8,128)(2,1)} %get-tuple-element.35), channel_id=1, source_target_pairs={{0,1},{1,0},{2,3},{3,2},{4,5},{5,4},{6,7},{7,6},{8,9},{9,8},{10,11... | collective-permute-start | bytes 3145736 | tf_op jit(solution)/shard_map/ppermute | solution.py:18
  705.8 62.1 %collective-permute-start.56 = (bf16[256,2048]{1,0:T(8,128)(2,1)}, bf16[256,2048]{1,0:T(8,128)(2,1)S(1)}, u32[]{:S(2)}, u32[]{:S(2)}) collective-permute-start(bf16[256,2048]{1,0:T(8,128)(2,1)} %get-tuple-element.39), channel_id=1, source_target_pairs={{0,2},{1,3},{2,0},{3,1},{4,6},{5,7},{6,4},{7,5},{8,10},{9,11},{10,... | collective-permute-start | bytes 3145736 | tf_op jit(solution)/shard_map/ppermute | solution.py:18
  707.3 60.6 %collective-permute-start.60 = (bf16[256,2048]{1,0:T(8,128)(2,1)}, bf16[256,2048]{1,0:T(8,128)(2,1)S(1)}, u32[]{:S(2)}, u32[]{:S(2)}) collective-permute-start(bf16[256,2048]{1,0:T(8,128)(2,1)} %fusion.67), channel_id=1, source_target_pairs={{0,4},{1,5},{2,6},{3,7},{4,0},{5,1},{6,2},{7,3},{8,12},{9,13},{10,... | collective-permute-start | bytes 3145736 | tf_op jit(solution)/shard_map/ppermute | solution.py:18
  728.4 42.4 %collective-permute-start.40 = (bf16[256,2048]{1,0:T(8,128)(2,1)}, bf16[256,2048]{1,0:T(8,128)(2,1)S(1)}, u32[]{:S(2)}, u32[]{:S(2)}) collective-permute-start(bf16[256,2048]{1,0:T(8,128)(2,1)} %get-tuple-element.41), channel_id=1, source_target_pairs={{0,1},{1,0},{2,3},{3,2},{4,5},{5,4},{6,7},{7,6},{8,9},{9,8},{10,11... | collective-permute-start | bytes 3145736 | tf_op jit(solution)/shard_map/ppermute | solution.py:18
  729.0 67.4 %collective-permute-start.42 = (bf16[256,2048]{1,0:T(8,128)(2,1)}, bf16[256,2048]{1,0:T(8,128)(2,1)S(1)}, u32[]{:S(2)}, u32[]{:S(2)}) collective-permute-start(bf16[256,2048]{1,0:T(8,128)(2,1)} %get-tuple-element.45), channel_id=1, source_target_pairs={{0,2},{1,3},{2,0},{3,1},{4,6},{5,7},{6,4},{7,5},{8,10},{9,11},{10,... | collective-permute-start | bytes 3145736 | tf_op jit(solution)/shard_map/ppermute | solution.py:18
  750.7 45.7 %collective-permute-start.46 = (bf16[256,2048]{1,0:T(8,128)(2,1)S(1)}, bf16[256,2048]{1,0:T(8,128)(2,1)S(1)}, u32[]{:S(2)}, u32[]{:S(2)}) collective-permute-start(bf16[256,2048]{1,0:T(8,128)(2,1)S(1)} %fusion.73), channel_id=1, source_target_pairs={{0,4},{1,5},{2,6},{3,7},{4,0},{5,1},{6,2},{7,3},{8,12},{9,13},{10,... | collective-permute-start | bytes 3145736 | tf_op jit(solution)/shard_map/ppermute | solution.py:18
  853.1 49.2 %collective-permute-start.93 = (bf16[2,256,2048]{2,1,0:T(8,128)(2,1)}, bf16[2,256,2048]{2,1,0:T(8,128)(2,1)}, u32[]{:S(2)}, u32[]{:S(2)}) collective-permute-start(bf16[2,256,2048]{2,1,0:T(8,128)(2,1)} %get-tuple-element.34), channel_id=1, source_target_pairs={{0,8},{8,0},{16,24},{24,16},{1,9},{9,1},{17,25},{25,17},{2,10},{10... | collective-permute-start | bytes 6291464 | tf_op jit(solution)/shard_map/ppermute | solution.py:18
  853.1 118.4 %collective-permute-start.92 = (bf16[2,256,2048]{2,1,0:T(8,128)(2,1)}, bf16[2,256,2048]{2,1,0:T(8,128)(2,1)}, u32[]{:S(2)}, u32[]{:S(2)}) collective-permute-start(bf16[2,256,2048]{2,1,0:T(8,128)(2,1)} %get-tuple-element.33), channel_id=1, source_target_pairs={{0,8},{8,0},{16,24},{24,16},{1,9},{9,1},{17,25},{25,17},{2,10},{10... | collective-permute-start | bytes 6291464 | tf_op jit(solution)/shard_map/ppermute | solution.py:18
  862.0 81.9 %collective-permute-start.90 = (bf16[2,512,2048]{2,1,0:T(8,128)(2,1)}, bf16[2,512,2048]{2,1,0:T(8,128)(2,1)}, u32[]{:S(2)}, u32[]{:S(2)}) collective-permute-start(bf16[2,512,2048]{2,1,0:T(8,128)(2,1)} %get-tuple-element.32), channel_id=1, source_target_pairs={{0,8},{8,0},{16,24},{24,16},{1,9},{9,1},{17,25},{25,17},{2,10},{10... | collective-permute-start | bytes 12582920 | tf_op jit(solution)/shard_map/ppermute | solution.py:18
  941.1 45.8 %collective-permute-start.94 = (bf16[2,256,2048]{2,1,0:T(8,128)(2,1)S(1)}, bf16[2,256,2048]{2,1,0:T(8,128)(2,1)S(1)}, u32[]{:S(2)}, u32[]{:S(2)}) collective-permute-start(bf16[2,256,2048]{2,1,0:T(8,128)(2,1)S(1)} %fusion.34), channel_id=1, source_target_pairs={{0,16},{8,24},{16,0},{24,8},{1,17},{9,25},{17,1},{25,9},{2,18},{10... | collective-permute-start | bytes 6291464 | tf_op jit(solution)/shard_map/ppermute | solution.py:18
  986.8 172.5 %collective-permute-start.89 = (bf16[2,512,2048]{2,1,0:T(8,128)(2,1)}, bf16[2,512,2048]{2,1,0:T(8,128)(2,1)}, u32[]{:S(2)}, u32[]{:S(2)}) collective-permute-start(bf16[2,512,2048]{2,1,0:T(8,128)(2,1)} %get-tuple-element.31), channel_id=1, source_target_pairs={{0,8},{8,0},{16,24},{24,16},{1,9},{9,1},{17,25},{25,17},{2,10},{10... | collective-permute-start | bytes 12582920 | tf_op jit(solution)/shard_map/ppermute | solution.py:18
  986.8 172.5 %collective-permute-start.91 = (bf16[2,512,2048]{2,1,0:T(8,128)(2,1)}, bf16[2,512,2048]{2,1,0:T(8,128)(2,1)}, u32[]{:S(2)}, u32[]{:S(2)}) collective-permute-start(bf16[2,512,2048]{2,1,0:T(8,128)(2,1)} %fusion.13), channel_id=1, source_target_pairs={{0,16},{8,24},{16,0},{24,8},{1,17},{9,25},{17,1},{25,9},{2,18},{10... | collective-permute-start | bytes 12582920 | tf_op jit(solution)/shard_map/ppermute | solution.py:18
  988.9 35.9 %collective-permute-start.70 = (bf16[4,64,1536]{2,1,0:T(8,128)(2,1)S(1)}, bf16[4,64,1536]{2,1,0:T(8,128)(2,1)S(1)}, u32[]{:S(2)}, u32[]{:S(2)}) collective-permute-start(bf16[4,64,1536]{2,1,0:T(8,128)(2,1)S(1)} %get-tuple-element.48), channel_id=1, source_target_pairs={{0,1},{1,0},{2,3},{3,2},{4,5},{5,4},{6,7},{7,6},{8,9},{9,8},{10,11... | collective-permute-start | bytes 2359304 | tf_op jit(solution)/shard_map/ppermute | solution.py:18
  989.5 36.8 %collective-permute-start.72 = (bf16[4,64,1536]{2,1,0:T(8,128)(2,1)S(1)}, bf16[4,64,1536]{2,1,0:T(8,128)(2,1)S(1)}, u32[]{:S(2)}, u32[]{:S(2)}) collective-permute-start(bf16[4,64,1536]{2,1,0:T(8,128)(2,1)S(1)} %fusion.93), channel_id=1, source_target_pairs={{0,2},{1,3},{2,0},{3,1},{4,6},{5,7},{6,4},{7,5},{8,10},{9,11},{10,... | collective-permute-start | bytes 2359304 | tf_op jit(solution)/shard_map/ppermute | solution.py:18
  1008.0 76.5 %collective-permute-start.67 = (bf16[4,64,1536]{2,1,0:T(8,128)(2,1)S(1)}, bf16[4,64,1536]{2,1,0:T(8,128)(2,1)S(1)}, u32[]{:S(2)}, u32[]{:S(2)}) collective-permute-start(bf16[4,64,1536]{2,1,0:T(8,128)(2,1)S(1)} %get-tuple-element.47), channel_id=1, source_target_pairs={{0,1},{1,0},{2,3},{3,2},{4,5},{5,4},{6,7},{7,6},{8,9},{9,8},{10,11... | collective-permute-start | bytes 2359304 | tf_op jit(solution)/shard_map/ppermute | solution.py:18
  1024.9 55.6 %collective-permute-start.88 = (f32[4352]{0:T(1024)S(1)}, f32[4352]{0:T(1024)S(1)}, u32[]{:S(2)}, u32[]{:S(2)}) collective-permute-start(f32[4352]{0:T(1024)S(1)} %add.368), channel_id=1, source_target_pairs={{0,16},{8,24},{16,0},{24,8},{1,17},{9,25},{17,1},{25,9},{2,18},{10... | collective-permute-start | bytes 52232 | tf_op jit(solution)/shard_map/ppermute | solution.py:18
  1026.9 57.7 %collective-permute-start.69 = (bf16[4,64,1536]{2,1,0:T(8,128)(2,1)S(1)}, bf16[4,64,1536]{2,1,0:T(8,128)(2,1)S(1)}, u32[]{:S(2)}, u32[]{:S(2)}) collective-permute-start(bf16[4,64,1536]{2,1,0:T(8,128)(2,1)S(1)} %get-tuple-element.51), channel_id=1, source_target_pairs={{0,2},{1,3},{2,0},{3,1},{4,6},{5,7},{6,4},{7,5},{8,10},{9,11},{10,... | collective-permute-start | bytes 2359304 | tf_op jit(solution)/shard_map/ppermute | solution.py:18
  1080.5 36.1 %collective-permute-start.73 = (bf16[4,64,1536]{2,1,0:T(8,128)(2,1)S(1)}, bf16[4,64,1536]{2,1,0:T(8,128)(2,1)S(1)}, u32[]{:S(2)}, u32[]{:S(2)}) collective-permute-start(bf16[4,64,1536]{2,1,0:T(8,128)(2,1)S(1)} %get-tuple-element.52), channel_id=1, source_target_pairs={{0,4},{1,5},{2,6},{3,7},{4,0},{5,1},{6,2},{7,3},{8,12},{9,13},{10,... | collective-permute-start | bytes 2359304 | tf_op jit(solution)/shard_map/ppermute | solution.py:18
  (112 other events, 3050.9 us)

commit v2 on v1

v2 whole, which is shorter than its diff:
```python
import functools
import math

import jax
import jax.numpy as jnp
from jax import lax
from jax.experimental import pallas as pl
from jax.experimental.pallas import tpu as pltpu
from jax.sharding import PartitionSpec as P

HEAD = 128
EPS = 1e-06
THETA = 10000.0
NEG = -1e30
LOW = jnp.bfloat16
F32 = jnp.float32
VMEM_LIMIT = 60 * 1024 * 1024


def swap(value, axis, mask):
    count = lax.axis_size(axis)
    return lax.ppermute(value, axis, [(i, i ^ mask) for i in range(count)])


def after(value, *others):
    return lax.optimization_barrier((value, *others))[0]


class Order:
    def __init__(self):
        self.last = None

    def __call__(self, *values):
        if self.last is not None:
            values = lax.optimization_barrier((*values, self.last))[:-1]
        self.last = values[0]
        return values if len(values) > 1 else values[0]

    def pin(self, value):
        return after(value, self.last)


class Gather:
    def __init__(self, order, shard, axis, gates=None):
        self.order, self.axis, self.got, self.gates = order, axis, {0: shard}, gates or {}
        count = lax.axis_size(axis)
        self.waiting = [1, 2, 4, 3, 6, 5, 7] if count == 8 else list(range(1, count))

    def take(self, count=None):
        ks, self.waiting = self.waiting[:count], self.waiting[count:] if count else []
        for k in ks:
            shard = self.got[k & (k - 1)]
            if k in self.gates:
                shard = after(shard, self.gates[k])
            self.got[k] = self.order(swap(shard, self.axis, k & -k))

    def take_to(self, k):
        self.take(self.waiting.index(k) + 1)

    def slots(self):
        return [self.got[k] for k in sorted(self.got)]

    def evens(self):
        return [self.got[k] for k in sorted(self.got) if k % 2 == 0]


def scatter_steps(r, top):
    bits = [1 << b for b in range(top.bit_length() - 1)]
    for bit in reversed(bits):
        yield from scatter_steps(r | bit, bit)
    for bit in bits:
        yield bit, r


class Scatter:
    def __init__(self, order, parts, axis, gates=None):
        self.order, self.axis, self.parts, self.gates = order, axis, list(parts), gates or {}
        self.waiting = list(scatter_steps(0, len(self.parts)))
        self.arrived = {}

    def take(self, count=None):
        steps, self.waiting = self.waiting[:count], self.waiting[count:] if count else []
        for bit, r in steps:
            sent = self.parts[r | bit].astype(LOW)
            before = self.arrived.setdefault(bit, [])
            if len(before) > 1:
                sent = after(sent, before[-2])
            if bit in self.gates:
                sent = after(sent, self.gates[bit])
            got = self.order(swap(sent, self.axis, bit))
            before.append(got)
            self.before, self.arrival = self.parts[r], got
            self.parts[r] = self.parts[r].astype(F32) + got.astype(F32)

    @property
    def total(self):
        return self.parts[0]


class Stack:
    def __init__(self, order, odd, even, axis, gates=None):
        self.order, self.axis, self.gates = order, axis, gates or {}
        self.bit, self.sent, self.terms = 1, odd, [(even, 1)]

    def take(self):
        gate = self.gates.get(self.bit)
        sent = self.sent if gate is None else after(self.sent, gate)
        got = self.order(swap(sent, self.axis, self.bit))
        self.bit, self.sent = 2 * self.bit, None
        self.terms.append((got, 1))
        if self.bit < lax.axis_size(self.axis):
            self.sent = sum(v[step :: 2 * step].astype(F32) for v, step in self.terms).astype(LOW)
            self.terms = [(v, 2 * step) for v, step in self.terms]

    def stacks(self):
        return [v for v, _ in self.terms]

    @property
    def total(self):
        return sum(v[0].astype(F32) for v in self.stacks())


class Sum:
    def __init__(self, order, value, axes):
        self.order, self.value = order, value
        self.waiting = [(a, 1 << b) for a in axes for b in range(lax.axis_size(a).bit_length() - 1)]

    def take(self, count=None):
        steps, self.waiting = self.waiting[:count], self.waiting[count:] if count else []
        for axis, bit in steps:
            self.value = self.value + self.order(swap(self.value, axis, bit))


def inv_rms(values):
    return lax.rsqrt(jnp.mean(values * values, axis=-1, keepdims=True) + EPS)


def norm_back(values, inv_scale, gain_vec, grad_in):
    scaled = grad_in * gain_vec
    mean_term = jnp.mean(scaled * values, axis=-1, keepdims=True)
    return inv_scale * scaled - values * (inv_scale * inv_scale * inv_scale) * mean_term


def rope_tables(slot_count):
    half_size = HEAD // 2
    frequency = THETA ** (-(jnp.arange(half_size, dtype=F32) * 2.0) / HEAD)
    angles = jnp.arange(slot_count, dtype=F32)[:, None] * frequency[None, :]
    cosine, sine = jnp.cos(angles), jnp.sin(angles)
    return jnp.concatenate([cosine, cosine], axis=1), jnp.concatenate([-sine, sine], axis=1)


def dot(a, b, contract=((1,), (0,))):
    return lax.dot_general(a, b, (contract, ((), ())), preferred_element_type=F32)


NT = ((1,), (1,))
TN = ((0,), (0,))


def call(kernel, grid, in_specs, out_specs, out_shape, flops, moved, scratch=(), prefetch=0, aliases=None):
    return pl.pallas_call(
        kernel,
        grid_spec=pltpu.PrefetchScalarGridSpec(
            num_scalar_prefetch=prefetch,
            grid=grid,
            in_specs=in_specs,
            out_specs=out_specs,
            scratch_shapes=list(scratch),
        ),
        out_shape=out_shape,
        input_output_aliases=aliases or {},
        compiler_params=pltpu.CompilerParams(vmem_limit_bytes=VMEM_LIMIT),
        cost_estimate=pl.CostEstimate(flops=flops, bytes_accessed=moved, transcendentals=0),
    )


def whole(dims):
    return pl.BlockSpec(dims, lambda *_: (0,) * len(dims), pipeline_mode=pl.Buffered(1))


def shape(dims, kind):
    return jax.ShapeDtypeStruct(dims, kind)


HBM = pl.BlockSpec(memory_space=pl.ANY)


def head_parts(raw, gain_vec, cosine, sine):
    scale = inv_rms(raw)
    normed = raw * scale * gain_vec
    rotated = normed * cosine + pltpu.roll(normed, HEAD // 2, axis=1) * sine
    return scale, rotated.astype(LOW)


def head_powers(query_rot, key_rot, values, length):
    scores = dot(query_rot, key_rot, NT)
    live = lax.broadcasted_iota(jnp.int32, scores.shape, 1) < length
    powers = jnp.where(live, jnp.exp(scores * (1.0 / math.sqrt(HEAD))), 0.0)
    sums = dot(powers.astype(LOW), jnp.concatenate([values, jnp.ones_like(values)], axis=1))
    inverse = 1.0 / sums[:, HEAD:]
    return powers, sums[:, :HEAD] * inverse, inverse


def attention_kernel(lens, xn, weight, gain, cosine, sine, proj, att, branch):
    length = lens[pl.program_id(0)]
    cols = att.shape[2]
    for part in range(3):
        proj[0, :, part * cols : (part + 1) * cols] = dot(xn[0], weight[:, part * cols : (part + 1) * cols])
    cos, sin = cosine[...], sine[...]
    for at in range(0, cols, HEAD):
        _, query_rot = head_parts(proj[0, :, at : at + HEAD], gain[0:1], cos, sin)
        _, key_rot = head_parts(proj[0, :, cols + at : cols + at + HEAD], gain[1:2], cos, sin)
        values = proj[0, :, 2 * cols + at : 2 * cols + at + HEAD].astype(LOW)
        att[0, :, at : at + HEAD] = head_powers(query_rot, key_rot, values, length)[1].astype(LOW)
    for c in range(branch.shape[2] // cols):
        block = weight[c * cols : (c + 1) * cols, 3 * cols :]
        branch[0, :, c * cols : (c + 1) * cols] = dot(att[0], block).astype(LOW)


def attention(lens, xn, weight, gain, cosine, sine):
    n_seq, slots, width = xn.shape
    cols = weight.shape[1] // 4
    one = lambda last: pl.BlockSpec((1, slots, last), lambda s, _: (s, 0, 0))
    return call(
        attention_kernel,
        (n_seq,),
        [one(width)] + [whole(v.shape) for v in (weight, gain, cosine, sine)],
        [one(3 * cols), one(cols), one(width)],
        [shape((n_seq, slots, 3 * cols), F32), shape((n_seq, slots, cols), LOW), shape(xn.shape, LOW)],
        flops=8 * n_seq * slots * width * cols,
        moved=weight.size * 2 + n_seq * slots * (4 * width + 14 * cols),
        prefetch=1,
    )(lens, xn, weight, gain, cosine, sine)


def attention_back_kernel(lens, grad, proj, xn, weight, gain, cosine, sine, grad_proj, grad_xn, grad_gain, grad_scaled):
    length = lens[pl.program_id(0)]
    cols = proj.shape[2] // 3
    factor = 1.0 / math.sqrt(HEAD)

    @pl.when(pl.program_id(0) == 0)
    def _():
        grad_gain[...] = jnp.zeros_like(grad_gain)
        grad_scaled[...] = jnp.zeros_like(grad_scaled)

    grad_att = jnp.zeros((grad.shape[1], cols), F32)
    for c in range(grad.shape[2] // cols):
        block = weight[c * cols : (c + 1) * cols, 3 * cols :]
        grad_att = grad_att + dot(grad[0, :, c * cols : (c + 1) * cols], block, NT)
    grad_att = grad_att.astype(LOW)
    cos, sin = cosine[...], sine[...]
    for at in range(0, cols, HEAD):
        query_raw = proj[0, :, at : at + HEAD]
        key_raw = proj[0, :, cols + at : cols + at + HEAD]
        query_scale, query_rot = head_parts(query_raw, gain[0:1], cos, sin)
        key_scale, key_rot = head_parts(key_raw, gain[1:2], cos, sin)
        values = proj[0, :, 2 * cols + at : 2 * cols + at + HEAD].astype(LOW)
        powers, attended, inverse = head_powers(query_rot, key_rot, values, length)
        probs = powers * jnp.concatenate([inverse] * (powers.shape[1] // HEAD), axis=1)
        grad_head = grad_att[:, at : at + HEAD]
        grad_probs = dot(grad_head, values, NT)
        grad_values = dot(probs.astype(LOW), grad_head, TN)
        inner = jnp.sum(attended * grad_head.astype(F32), axis=-1, keepdims=True)
        grad_scores = (probs * (grad_probs - inner)).astype(LOW)
        grad_qrot = dot(grad_scores, key_rot) * factor
        grad_krot = dot(grad_scores, query_rot, TN) * factor
        grad_qnorm = grad_qrot * cos - pltpu.roll(grad_qrot, HEAD // 2, axis=1) * sin
        grad_knorm = grad_krot * cos - pltpu.roll(grad_krot, HEAD // 2, axis=1) * sin
        grad_query = norm_back(query_raw, query_scale, gain[0:1], grad_qnorm)
        grad_key = norm_back(key_raw, key_scale, gain[1:2], grad_knorm)
        grad_gain[0:1] += jnp.sum(grad_qnorm * query_raw * query_scale, axis=0, keepdims=True)
        grad_gain[1:2] += jnp.sum(grad_knorm * key_raw * key_scale, axis=0, keepdims=True)
        for part, value in enumerate((grad_query, grad_key, grad_values)):
            grad_proj[0, :, part * cols + at : part * cols + at + HEAD] = value.astype(LOW)
    for c in range(grad_xn.shape[2] // cols):
        rows = slice(c * cols, (c + 1) * cols)
        block = dot(grad_proj[0], weight[rows, : 3 * cols], NT)
        grad_xn[0, :, rows] = block.astype(LOW)
        grad_scaled[0:1, rows] += jnp.sum(block * xn[0, :, rows].astype(F32), axis=0, keepdims=True)


def attention_back(lens, grad, proj, xn, weight, gain, cosine, sine):
    n_seq, slots, width = grad.shape
    cols = weight.shape[1] // 4
    one = lambda last: pl.BlockSpec((1, slots, last), lambda s, _: (s, 0, 0))
    return call(
        attention_back_kernel,
        (n_seq,),
        [one(width), one(3 * cols), one(width)] + [whole(v.shape) for v in (weight, gain, cosine, sine)],
        [one(3 * cols), one(width)] + [pl.BlockSpec((8, last), lambda s, _: (0, 0)) for last in (HEAD, width)],
        [
            shape((n_seq, slots, 3 * cols), LOW),
            shape(grad.shape, LOW),
            shape((8, HEAD), F32),
            shape((8, width), F32),
        ],
        flops=8 * n_seq * slots * width * cols,
        moved=weight.size * 2 + n_seq * slots * (6 * width + 18 * cols),
        prefetch=1,
    )(lens, grad, proj, xn, weight, gain, cosine, sine)


def attention_weight_kernel(me, xn, grad_proj, att, grad, out):
    first = dot(xn[...], grad_proj[...], TN)
    second = dot(att[...], grad[...], TN)
    n_ep, rows = out.shape[0], out.shape[2]
    for j in range(n_ep):
        out[me[0] ^ j, 0, :, : first.shape[1]] = first[j * rows : (j + 1) * rows].astype(LOW)
        out[me[0] ^ j, 0, :, first.shape[1] :] = second[j * rows : (j + 1) * rows].astype(LOW)


def attention_weight_grad(me, xn, grad_proj, att, grad, n_ep):
    rows, width = xn.shape
    cols = att.shape[1]
    n_dp = width // cols
    strip = pl.BlockSpec((rows, cols), lambda i, _: (0, i))
    out = (n_ep, n_dp, cols // n_ep, 4 * cols)
    return call(
        attention_weight_kernel,
        (n_dp,),
        [strip, whole(grad_proj.shape), whole(att.shape), strip],
        pl.BlockSpec((n_ep, 1, cols // n_ep, 4 * cols), lambda i, _: (0, i, 0, 0)),
        shape(out, LOW),
        flops=8 * rows * width * cols,
        moved=rows * (4 * width + 8 * cols) + 8 * width * cols,
        prefetch=1,
    )(me, xn, grad_proj, att, grad)


def place_kernel(me, share, *refs):
    *pieces, out = refs
    n_dp, rows, _ = share.shape
    cols = share.shape[2] // 4
    width = n_dp * cols
    for r in range(n_dp):
        block = me[0] ^ r
        piece = pieces[r - 1][...].astype(F32) if r else share[block, :, : 3 * cols]
        for part in range(3):
            at = pl.multiple_of(part * width + block * cols, HEAD)
            out[:, pl.ds(at, cols)] = piece[:, part * cols : (part + 1) * cols]
        out[:, 3 * width + r * cols : 3 * width + (r + 1) * cols] = share[r, :, 3 * cols :]


def place_share(me, share, pieces):
    n_dp, rows, last = share.shape
    out = (rows, n_dp * last)
    return call(
        place_kernel,
        (1,),
        [whole(share.shape)] + [whole(p.shape) for p in pieces],
        pl.BlockSpec(out, lambda *_: (0, 0)),
        shape(out, F32),
        flops=0,
        moved=share.size * 10,
        prefetch=1,
    )(me, share, *pieces)


def one_hot(places, seats, axis):
    experts, slots = places.shape if axis == 0 else places.shape[::-1]
    dims = (experts * seats, slots) if axis == 0 else (slots, experts * seats)
    index = lax.broadcasted_iota(jnp.int32, dims, axis).astype(F32)
    hit = None
    for e in range(experts):
        spot = places[e : e + 1] if axis == 0 else places[:, e : e + 1]
        hit = (index == spot) if hit is None else hit | (index == spot)
    return hit.astype(LOW)


def seat_weights(places, weights, seats):
    experts, slots = places.shape
    index = lax.broadcasted_iota(jnp.int32, (experts * seats, slots), 0).astype(F32)
    total = jnp.zeros(index.shape, F32)
    for e in range(experts):
        total = jnp.where(index == places[e : e + 1], weights[e : e + 1], total)
    return jnp.sum(total, axis=1, keepdims=True)


def picked(out, place, xs, seats, weights=None):
    for s, x in enumerate(xs):
        rows = dot(one_hot(place[s], seats, 0), x[...])
        if weights is not None:
            rows = rows * seat_weights(place[s], weights[s], seats)
        for e in range(out.shape[0]):
            out[e, s * seats : (s + 1) * seats] = rows[e * seats : (e + 1) * seats].astype(LOW)


STRIP = 256


def grad_in_kernel(n_xs, seats, place, weights, *refs):
    xs, (down, grad_rows, grad_act) = refs[:n_xs], refs[n_xs:]

    @pl.when(pl.program_id(0) == 0)
    def _():
        picked(grad_rows, place, xs, seats, weights)

    for e in range(down.shape[0]):
        grad_act[e] = dot(grad_rows[e], down[e], NT).astype(LOW)


def grad_in(seats, place, weights, xs, down):
    experts, hidden, width = down.shape
    rows = len(xs) * seats
    return call(
        functools.partial(grad_in_kernel, len(xs), seats),
        (hidden // STRIP,),
        [whole(place.shape), whole(weights.shape)]
        + [whole(x.shape) for x in xs]
        + [pl.BlockSpec((experts, STRIP, width), lambda n: (0, n, 0))],
        [
            pl.BlockSpec((experts, rows, width), lambda n: (0, 0, 0)),
            pl.BlockSpec((experts, rows, STRIP), lambda n: (0, 0, n)),
        ],
        [shape((experts, rows, width), LOW), shape((experts, rows, hidden), LOW)],
        flops=2 * experts * rows * width * (hidden + xs[0].shape[0]),
        moved=down.size * 2 + experts * rows * (width + hidden) * 2,
    )(place, weights, *xs, down)


def gate_up_kernel(n_xs, seats, place, *refs):
    xs, (gate_w, up_w, grad_act) = refs[:n_xs], refs[n_xs : n_xs + 3]
    rows, activation, grad_gu = refs[-3:]

    @pl.when(pl.program_id(0) == 0)
    def _():
        picked(rows, place, xs, seats)

    for e in range(gate_w.shape[0]):
        gate = dot(rows[e], gate_w[e])
        up = dot(rows[e], up_w[e])
        sigmoid = jax.nn.sigmoid(gate)
        silu = gate * sigmoid
        grad = grad_act[e].astype(F32)
        activation[e] = (silu * up).astype(LOW)
        grad_gu[e, 0] = (grad * up * sigmoid * (1.0 + gate * (1.0 - sigmoid))).astype(LOW)
        grad_gu[e, 1] = (grad * silu).astype(LOW)


def gate_up(group, total, seats, place, xs, weight, grad_act, kept):
    experts, width, both = weight.shape
    hidden = both // 2
    rows = len(xs) * seats
    steps = hidden // STRIP
    outs = [
        shape((experts, total, width), LOW),
        shape((experts, total, hidden), LOW),
        shape((experts, 2, total, hidden), LOW),
    ]
    n_in = 4 + len(xs)
    return call(
        functools.partial(gate_up_kernel, len(xs), seats),
        (steps,),
        [whole(place.shape)]
        + [whole(x.shape) for x in xs]
        + [
            pl.BlockSpec((experts, width, STRIP), lambda n: (0, 0, n)),
            pl.BlockSpec((experts, width, STRIP), lambda n: (0, 0, n + steps)),
            pl.BlockSpec((experts, rows, STRIP), lambda n: (0, group, n)),
        ]
        + [HBM] * len(kept),
        [
            pl.BlockSpec((experts, rows, width), lambda n: (0, group, 0)),
            pl.BlockSpec((experts, rows, STRIP), lambda n: (0, group, n)),
            pl.BlockSpec((experts, 2, rows, STRIP), lambda n: (0, 0, group, n)),
        ],
        outs,
        flops=2 * experts * rows * width * (both + xs[0].shape[0]),
        moved=weight.size * 2 + experts * rows * (width + 2 * both) * 2,
        aliases={n_in + i: i for i in range(len(kept))},
    )(place, *xs, weight, weight, grad_act, *kept)


def combine_kernel(seats, dest, place, weights, spots, rows, weight, *refs):
    outs, (block, hot, scale) = refs[:-3], refs[-3:]
    n_xs, experts = spots.shape[0], rows.shape[0]
    apply = len(rows.shape) == 3

    @pl.when(pl.program_id(0) == 0)
    def _():
        for s in range(n_xs):
            hot[s] = one_hot(spots[s], seats, 1)
            if apply:
                scale[s] = seat_weights(place[s], weights[s], seats)

    for e in range(experts):
        if apply:
            result = dot(rows[e], weight[e])
        else:
            depth = rows.shape[3]
            result = dot(rows[e, 0], weight[e, :, :depth], NT) + dot(rows[e, 1], weight[e, :, depth:], NT)
        for s in range(n_xs):
            part = result[s * seats : (s + 1) * seats]
            if apply:
                part = part * scale[s, e * seats : (e + 1) * seats]
            block[s, e * seats : (e + 1) * seats] = part.astype(LOW)
    for s, (out, i) in enumerate(dest):
        outs[out][i] = dot(hot[s], block[s]).astype(LOW)


def combine(group, seats, dest, place, weights, rows, weight):
    experts, depth = rows.shape[0], rows.shape[-1]
    n_xs, _, slots = place.shape
    n_rows, strip = n_xs * seats, 512
    if rows.ndim == 3:
        width = weight.shape[2]
        row_spec = pl.BlockSpec((experts, n_rows, depth), lambda n: (0, group, 0))
        weight_spec = pl.BlockSpec((experts, depth, strip), lambda n: (0, 0, n))
    else:
        width = weight.shape[1]
        row_spec = pl.BlockSpec((experts, 2, n_rows, depth), lambda n: (0, 0, group, 0))
        weight_spec = pl.BlockSpec((experts, strip, 2 * depth), lambda n: (0, n, 0))
    spots = place.transpose(0, 2, 1)
    counts = [sum(1 for out, _ in dest if out == i) for i in range(1 + max(out for out, _ in dest))]
    return call(
        functools.partial(combine_kernel, seats, dest),
        (width // strip,),
        [whole(place.shape), whole(weights.shape), whole(spots.shape), row_spec, weight_spec],
        [pl.BlockSpec((count, slots, strip), lambda n: (0, 0, n)) for count in counts],
        [shape((count, slots, width), LOW) for count in counts],
        flops=2 * experts * n_rows * width * (depth * (rows.ndim - 2) + slots),
        moved=weight.size * 2 + experts * n_rows * depth * (rows.ndim - 2) * 2 + n_xs * slots * width * 2,
        scratch=[
            pltpu.VMEM((n_xs, experts * seats, strip), LOW),
            pltpu.VMEM((n_xs, slots, experts * seats), LOW),
            pltpu.VMEM((n_xs, experts * seats, 1), F32),
        ],
    )(place, weights, spots, rows, weight)


def expert_grad_kernel(me, rows, grad_gu, activation, grad_rows, send, keep):
    first, hidden = rows.shape[2], grad_gu.shape[3]

    def fill(out):
        for part in range(2):
            out[0, :first, part * hidden : (part + 1) * hidden] = dot(rows[0], grad_gu[0, part], TN).astype(LOW)
        out[0, first:] = dot(activation[0], grad_rows[0], TN).astype(LOW)

    pl.when(pl.program_id(0) < pl.num_programs(0) // 2)(functools.partial(fill, send))
    pl.when(pl.program_id(0) >= pl.num_programs(0) // 2)(functools.partial(fill, keep))


def expert_grad(e, me, rows, grad_gu, activation, grad_rows, n_dp):
    n_rows, width = rows.shape[1:]
    hidden = activation.shape[2]
    first, second, half = width // n_dp, hidden // n_dp, n_dp // 2
    rank = lambda i: jnp.where(i < half, 2 * i + 1, 2 * (i - half))
    strip = lambda last: pl.BlockSpec((1, n_rows, last), lambda i, me: (e, 0, rank(i) ^ me[0]))
    one = lambda *dims: pl.BlockSpec((1, *dims), lambda i, me: (e,) + (0,) * len(dims), pipeline_mode=pl.Buffered(1))
    out = (first + second, width)
    return call(
        expert_grad_kernel,
        (n_dp,),
        [strip(first), one(2, n_rows, hidden), strip(second), one(n_rows, width)],
        [
            pl.BlockSpec((1, *out), lambda i, me: (jnp.minimum(i, half - 1), 0, 0)),
            pl.BlockSpec((1, *out), lambda i, me: (jnp.maximum(i - half, 0), 0, 0)),
        ],
        [shape((half, *out), LOW)] * 2,
        flops=2 * n_rows * width * 3 * hidden,
        moved=n_rows * (2 * width + 3 * hidden) * 2 + 3 * hidden * width * 2,
        prefetch=1,
    )(me, rows, grad_gu, activation, grad_rows)


def finish_kernel(n_terms, *refs):
    terms, (first, second) = refs[:n_terms], refs[-2:]
    rows = first.shape[1]
    total = terms[0][0].astype(F32)
    for term in terms[1:]:
        total = total + term[0].astype(F32)
    first[0] = total[:rows]
    second[0] = total[rows:]


def finish(e, experts, first, terms, kept):
    _, rows, width = terms[0].shape
    strip = 512
    outs = [shape((experts, first, width), F32), shape((experts, rows - first, width), F32)]
    return call(
        functools.partial(finish_kernel, len(terms)),
        (width // strip,),
        [pl.BlockSpec((1, rows, strip), lambda n: (0, 0, n))] * len(terms) + [HBM] * len(kept),
        [pl.BlockSpec((1, v.shape[1], strip), lambda n: (e, 0, n)) for v in outs],
        outs,
        flops=rows * width,
        moved=rows * width * (4 + 2 * len(terms)),
        aliases={len(terms) + i: i for i in range(len(kept))},
    )(*terms, *kept)


def on_device(
    tokens,
    lengths,
    routes,
    pair_order,
    gate_weights,
    attn_weight,
    gains,
    expert_gate_up,
    expert_down,
    cotangent,
):
    slot_count, width = tokens.shape[1:]
    top_count = routes.shape[2]
    experts_dev, hidden = expert_down.shape[:2]
    rows_dev = attn_weight.shape[0]
    n_dp, n_ep = lax.axis_size("dp"), lax.axis_size("ep")
    my_dp, my_ep = lax.axis_index("dp"), lax.axis_index("ep")
    at_dp, at_ep = my_dp.reshape(1), my_ep.reshape(1)
    experts = experts_dev * n_ep
    capacity = (9 * slot_count * top_count + 8 * experts - 1) // (8 * experts)
    seats = (capacity + 15) // 16 * 16
    cols = width // n_dp

    order = Order()
    inputs = tokens[0].astype(F32)
    length = lengths[0]
    gain_attn = gains[:width]
    gain_ffn = gains[width : 2 * width]
    gain_head = gains[2 * width :].reshape(2, HEAD)
    cosine, sine = rope_tables(slot_count)

    out_in = Gather(order, cotangent[0], "ep")
    out_in.take(2)

    slot_live = jnp.arange(slot_count) < length
    live_rows = slot_live.astype(F32)[:, None]
    named = routes[0][:, :, None] == jnp.arange(experts, dtype=jnp.int32)
    rank_of = pair_order[0].reshape(slot_count, top_count)[:, :, None]
    rank_of = jnp.sum(jnp.where(named, rank_of, 0), axis=1).T
    weight_of = jnp.sum(jnp.where(named, gate_weights[0][:, :, None], 0.0), axis=1).T
    live_pair = jnp.any(named, axis=1).T & slot_live[None, :]
    earlier = live_pair[:, :, None] & (rank_of[:, :, None] < rank_of[:, None, :])
    pair_rank = jnp.sum(earlier.astype(jnp.int32), axis=1)
    kept = live_pair & (pair_rank < capacity)
    place = jnp.where(kept, pair_rank.astype(F32), -1.0)
    weight_of = jnp.where(kept, weight_of, 0.0)
    weight_high = weight_of.astype(LOW)
    weight_low = (weight_of - weight_high.astype(F32)).astype(LOW)
    extra = jnp.concatenate([place.astype(LOW), weight_high, weight_low]).reshape(-1, 4 * cols)
    n_extra = extra.shape[0]
    extra = jnp.pad(extra, ((0, -n_extra % 16), (0, 0)))

    last = attn_weight[:, 3 * width :].reshape(rows_dev, n_dp, cols).transpose(1, 0, 2)
    shard = jnp.concatenate([jnp.zeros((n_dp, rows_dev, 3 * cols), LOW), last], axis=2)
    for r in reversed(range(n_dp)):
        block = my_dp ^ r
        piece = jnp.concatenate(
            [
                lax.dynamic_slice(attn_weight, (0, part * width + block * cols), (rows_dev, cols))
                for part in range(3)
            ],
            axis=1,
        )
        piece = swap(piece, "dp", r) if r else piece
        shard = lax.dynamic_update_slice(shard, piece[None], (block, 0, 0))
    shard = order(jnp.concatenate([shard.reshape(-1, 4 * cols), extra]))
    weights_in = Gather(order, shard, "ep")
    lens_in = Gather(order, order.pin(lengths), "dp")
    scale_first = inv_rms(inputs)
    xn_in = Gather(order, order.pin((inputs * scale_first * gain_attn).astype(LOW)), "dp")
    lens_in.take()
    xn_in.take(1)
    weights_in.take(2)
    xn_in.take(1)
    weights_in.take(2)
    xn_in.take()
    weights_in.take(n_ep - 6)
    out_in.gates = {4: order.last}
    weights_in.take(1)
    out_in.gates.update({k: order.last for k in out_in.waiting if k & (k - 1) == 2})
    weights_in.take()
    weight = jnp.zeros((n_dp, n_ep, rows_dev, 4 * cols), LOW)
    for s, part in sorted(weights_in.got.items()):
        part = part[: n_dp * rows_dev].reshape(n_dp, 1, rows_dev, 4 * cols)
        weight = lax.dynamic_update_slice(weight, part, (0, my_ep ^ s, 0, 0))
    weight = weight.reshape(width, 4 * cols)

    xn_first = jnp.stack(xn_in.slots())
    lens = order.pin(jnp.concatenate(lens_in.slots()))
    proj, attended, branch = order(*attention(lens, xn_first, weight, gain_head, cosine, sine))
    branch_sum = Scatter(order, list(branch), "dp")
    out_in.take_to(4)
    branch_sum.take(1)
    out_in.take(1)
    branch_sum.take()
    resid = inputs + branch_sum.total
    scale_second = inv_rms(resid)
    xn_second = order((resid * scale_second * gain_ffn).astype(LOW))

    x_in = Gather(order, xn_second, "ep")
    late = [n_ep - 3, n_ep - 1]
    early = [k for k in range(n_ep) if k not in late]
    ranked = early + late
    out_in.take(n_ep - 6)
    x_in.take(1)
    out_in.take()
    meta = jnp.stack([weights_in.got[k][n_dp * rows_dev :][:n_extra] for k in ranked])
    meta = meta.reshape(n_ep, 3, experts, slot_count).astype(F32)
    meta = lax.dynamic_slice_in_dim(meta, my_ep * experts_dev, experts_dev, axis=2)
    weight_in = meta[:, 1] + meta[:, 2]
    first_seat = jnp.arange(experts_dev, dtype=F32)[None, :, None] * seats
    place_in = jnp.where(meta[:, 0] < 0.0, -1.0, meta[:, 0] + first_seat)
    groups = [(0, slice(0, n_ep - 2), early), (n_ep // 2 - 1, slice(n_ep - 2, n_ep), late)]
    n_rows = n_ep * seats
    grad_rows, grad_act = order(
        *grad_in(seats, order.pin(place_in), weight_in, [out_in.got[k] for k in ranked], expert_down)
    )
    while any(k in x_in.waiting for k in early):
        x_in.take(1)
    backs = {}

    def forward_group(g, forward):
        at, h, ks = groups[g]
        xs = [x_in.got[k] for k in ks]
        return order(*gate_up(at, n_rows, seats, order.pin(place_in[h]), xs, expert_gate_up, grad_act, forward))

    def back_group(g):
        at, h, ks = groups[g]
        dest = [(i, 0) for i in range(len(ks))]
        terms = combine(at, seats, dest, order.pin(place_in[h]), weight_in[h], grad_gu, expert_gate_up)
        backs.update(zip(ks, [term[0] for term in order(*terms)], strict=True))

    forward = forward_group(0, [])
    x_in.take()
    rows, activation, grad_gu = forward_group(1, forward)
    back_group(1)
    back_group(0)
    back_sum = Scatter(order, [backs[k] for k in range(n_ep)], "ep")

    def expert_sum(e):
        terms = expert_grad(e, order.pin(at_dp), rows, grad_gu, activation, grad_rows, n_dp)
        return Stack(order, *order(*terms), "dp")

    back_sum.take(1)
    sums = [expert_sum(0)]
    back_sum.take(n_ep - 5)
    dest = [(1 - k % 2, k // 2) for k in ranked]
    mixes = order(*combine(0, seats, dest, order.pin(place_in), weight_in, activation, expert_down))
    back_sum.take(1)
    mixed = Stack(order, *mixes, "ep", {1: order.last})
    back_sum.take()
    grad_xn_second = back_sum.total

    grad_out = cotangent[0].astype(F32) * live_rows
    grad_resid = grad_out + norm_back(resid, scale_second, gain_ffn, grad_xn_second)
    grad_gain_ffn = jnp.sum(grad_xn_second * resid * scale_second, axis=0)
    grad_shard, grad_gain_ffn = order(grad_resid.astype(LOW), grad_gain_ffn)
    grad_in_dp = Gather(order, grad_shard, "dp")
    grad_in_dp.take(1)
    sums += [expert_sum(e) for e in range(1, experts_dev)]
    grad_in_dp.take()
    sums[0].take()
    sums[0].gates = {2: order.last}
    grad_branch = jnp.stack(grad_in_dp.slots())
    grad_proj, grad_xn, grad_gain_head, grad_scaled = order(
        *attention_back(order.pin(lens), grad_branch, proj, xn_first, weight, gain_head, cosine, sine)
    )
    grad_gain_attn = grad_scaled[0] / gain_attn
    gain_terms = jnp.concatenate([grad_gain_attn, grad_gain_ffn, grad_gain_head[0], grad_gain_head[1]])
    gain_sum = Sum(order, gain_terms, ("ep", "dp"))
    xn_sum = Scatter(order, list(grad_xn), "dp")
    xn_sum.take(1)
    flat = lambda v: v.reshape(n_dp * slot_count, -1)
    terms = order(
        attention_weight_grad(
            order.pin(at_ep), flat(xn_first), flat(grad_proj), flat(attended), flat(grad_branch), n_ep
        )
    )
    weight_sum = Scatter(order, list(terms), "ep")
    mixed.take()
    gain_sum.take(1)
    for total in sums[1:]:
        total.take()
    xn_sum.take()
    for total in sums[1:]:
        total.gates = {2: order.last}
    grad_xn_first = xn_sum.total
    input_grad = order(grad_resid + norm_back(inputs, scale_first, gain_attn, grad_xn_first))
    weight_sum.take(1)
    gain_sum.take(1)
    while mixed.sent is not None:
        mixed.take()
    output = order((live_rows * (resid + mixed.total)).astype(LOW))
    gain_sum.take(1)
    weight_sum.take(1)
    expert_grads = []
    for e, total in enumerate(sums):
        if e == len(sums) - 1:
            weight_sum.take(n_ep - 4)
            gain_sum.take()
            weight_sum.take()
            share = weight_sum.total
            pieces = []
            for r in range(1, n_dp):
                piece = lax.dynamic_index_in_dim(share, my_dp ^ r, axis=0, keepdims=False)
                pieces.append(swap(piece[:, : 3 * cols].astype(LOW), "dp", r))
        while total.sent is not None:
            total.take()
        expert_grads = order(*finish(e, experts_dev, width // n_dp, total.stacks(), expert_grads))
    gate_up_grad, down_grad = expert_grads
    attn_share = place_share(at_dp, share, pieces)
    gain_part = gain_terms.shape[0] // (n_dp * n_ep)
    gain_share = lax.dynamic_slice_in_dim(gain_sum.value, (my_dp * n_ep + my_ep) * gain_part, gain_part)
    return (output[None], input_grad[None], attn_share, gain_share, gate_up_grad, down_grad)


def solution(mesh):
    in_specs = (
        P(("dp", "ep"), None, None),
        P(("dp", "ep")),
        P(("dp", "ep"), None, None),
        P(("dp", "ep"), None),
        P(("dp", "ep"), None, None),
        P(("dp", "ep"), None),
        P(),
        P("ep", None, None),
        P("ep", None, None),
        P(("dp", "ep"), None, None),
    )
    out_specs = (
        P(("dp", "ep"), None, None),
        P(("dp", "ep"), None, None),
        P(("dp", "ep"), None),
        P(("dp", "ep")),
        P("ep", "dp", None),
        P("ep", "dp", None),
    )
    return jax.shard_map(
        on_device, mesh=mesh, in_specs=in_specs, out_specs=out_specs, check_vma=False
    )
```

time: 1180 us -> 862 us (0.73)
  Pallas kernels: 0 us -> 250 us
  matrix products: 214 us -> 0 us
  waiting for transfers between devices: 611 us -> 397 us
  local copies, waits for them, and re-layouts: 171 us -> 55.9 us
  other arithmetic: 98.8 us -> 70.6 us
    pallas_call x0 -> x14, Pallas kernels: none -> 250 us  [the longest x3 57.3 us: combine(): call(functools.partial(combine_kernel, seats, dest), (width // strip,), [...]
    dot_general x22 -> x0, matrix products: 214 us -> none  [the longest x1 29.5 us: on_device(): jnp.einsum('sjcd,sjcf->jdf', received, grad_gate_up, preferred_element_ty...]
    ppermute x95 -> x68, waiting for transfers between devices: 611 us -> 397 us  [swap(): return lax.ppermute(value, axis, [(i, i ^ mask) for i in range(count)])]
    dynamic_update_slice x24 -> x11, local copies, waits for them, and re-layouts: 49.6 us -> 8.48 us  [the longest x8 8.43 us: on_device(): weight = lax.dynamic_update_slice(weight, part, (0, my_ep ^ s, 0, 0))]
    unnamed x153 -> x91, local copies, waits for them, and re-layouts: 36.2 us -> 7.2 us
    slice x3 -> x35, local copies, waits for them, and re-layouts: 4.58 us -> 17.6 us  [the longest x4 6.28 us: back_group(): weight_in[h]]
    squeeze x4 -> x2, local copies, waits for them, and re-layouts: 13.1 us -> 0.86 us  [the longest x1 0.75 us: on_device(): grad_gain_head[0]]
    ppermute x95 -> x68, starting transfers between devices: 73.4 us -> 74.9 us  [swap(): return lax.ppermute(value, axis, [(i, i ^ mask) for i in range(count)])]
  transfers between devices with their start and end apart: 95 -> 68, of which waited for: 45 -> 35; matrix products, arithmetic and copies ran while one was open for 28% -> 14% of each run, Pallas kernels for 0% -> 26%
where the time goes in v2:
time: 862 us; the launch traced here: 851 us
  waiting for transfers between devices  397 us (46%)
  Pallas kernels  250 us (29%)
  starting transfers between devices  74.9 us (9%)
  other arithmetic  70.6 us (8%)
  local copies, waits for them, and re-layouts  55.9 us (6%)
    ppermute x68, waiting for transfers between devices, swap(): return lax.ppermute(value, axis, [(i, i ^ mask) for i in range(count)])  397 us
    ppermute x68, starting transfers between devices, swap(): return lax.ppermute(value, axis, [(i, i ^ mask) for i in range(count)])  74.9 us
    pallas_call x3, Pallas kernels, combine(): call(functools.partial(combine_kernel, seats, dest), (width // strip,), [...  57.3 us
    pallas_call x2, Pallas kernels, expert_grad(): call(expert_grad_kernel, (n_dp,), [strip(first), one(2, n_rows, hidden),...  48.6 us
    pallas_call x2, Pallas kernels, gate_up(): call(functools.partial(gate_up_kernel, len(xs), seats), (steps,), [whole(...  41.2 us
    pallas_call x1, Pallas kernels, attention_back(): call(attention_back_kernel, (n_seq,), [one(width), one(3 * cols), one(wid...  34.3 us
    pallas_call x1, Pallas kernels, grad_in(): call(functools.partial(grad_in_kernel, len(xs), seats), (hidden // STRIP,...  19.8 us
    pallas_call x1, Pallas kernels, attention(): call(attention_kernel, (n_seq,), [one(width)] + [whole(v.shape) for v in...  18.1 us
  transfers between devices with their start and end apart: 68, of which 35 were waited for; matrix products, arithmetic and copies ran while one was open for 14% of the time, Pallas kernels for 26%

profile of v2, /device:TPU:0, one launch (start us, length us, event | category | flops | bytes accessed | tf_op | source)
XLA Modules:
  0.0 851.1 jit_solution(9727253239085064751)
XLA Ops:
  13.7 4.3 collective-permute-done.1
  18.2 9.0 %collective-permute-done.4.refs_1_ = bf16[256,2048]{1,0:T(8,128)(2,1)} collective-permute-done((bf16[256,2048]{1,0:T(8,128)(2,1)}, bf16[256,2048]{1,0:T(8,128)(2,1)}, u32[]{:S(2)}, u32[]{:S(2)}) %collective-permute-start.4) | collective-permute-done | bytes 1048608 | tf_op jit(solution)/shard_map/ppermute | solution.py:22
  43.0 10.7 %collective-permute-done.11 = bf16[272,2048]{1,0:T(8,128)(2,1)S(1)} collective-permute-done((bf16[272,2048]{1,0:T(8,128)(2,1)S(1)}, bf16[272,2048]{1,0:T(8,128)(2,1)S(1)}, u32[]{:S(2)}, u32[]{:S(2)}) %collective-permute-start.11) | collective-permute-done | bytes 1114144 | tf_op jit(solution)/shard_map/ppermute | solution.py:22
  53.7 24.3 %collective-permute-done.10 = bf16[272,2048]{1,0:T(8,128)(2,1)} collective-permute-done((bf16[272,2048]{1,0:T(8,128)(2,1)S(1)}, bf16[272,2048]{1,0:T(8,128)(2,1)}, u32[]{:S(2)}, u32[]{:S(2)}) %collective-permute-start.10) | collective-permute-done | bytes 1114144 | tf_op jit(solution)/shard_map/ppermute | solution.py:22
  83.7 4.5 broadcast_in_dim.90
  96.5 9.4 %collective-permute-done.15 = bf16[272,2048]{1,0:T(8,128)(2,1)} collective-permute-done((bf16[272,2048]{1,0:T(8,128)(2,1)}, bf16[272,2048]{1,0:T(8,128)(2,1)}, u32[]{:S(2)}, u32[]{:S(2)}) %collective-permute-start.15) | collective-permute-done | bytes 1114144 | tf_op jit(solution)/shard_map/ppermute | solution.py:22
  107.2 19.3 %collective-permute-done.17 = bf16[272,2048]{1,0:T(8,128)(2,1)S(1)} collective-permute-done((bf16[272,2048]{1,0:T(8,128)(2,1)}, bf16[272,2048]{1,0:T(8,128)(2,1)S(1)}, u32[]{:S(2)}, u32[]{:S(2)}) %collective-permute-start.17) | collective-permute-done | bytes 1114144 | tf_op jit(solution)/shard_map/ppermute | solution.py:22
  138.0 13.9 %collective-permute-done.16 = bf16[272,2048]{1,0:T(8,128)(2,1)S(1)} collective-permute-done((bf16[272,2048]{1,0:T(8,128)(2,1)}, bf16[272,2048]{1,0:T(8,128)(2,1)S(1)}, u32[]{:S(2)}, u32[]{:S(2)}) %collective-permute-start.16) | collective-permute-done | bytes 1114144 | tf_op jit(solution)/shard_map/ppermute | solution.py:22
  153.2 18.1 %shard_map.145 = (f32[4,256,1536]{2,1,0:T(8,128)}, bf16[4,256,512]{2,1,0:T(8,128)(2,1)}, bf16[4,256,2048]{2,1,0:T(8,128)(2,1)}) custom-call(s32[4]{0:T(128)} %pad_add_fusion.lens, bf16[4,256,2048]{2,1,0:T(8,128)(2,1)} %pad_maximum_fusion.xn, bf16[2048,2048]{1,0:T(8,128)(2,1)} %bitcast.35.weight, f32[2,128]{1,0:T(2,128)} %slice_bitcast_fusion.10.gain, ...), custom_call_target="tpu_custom_call" | custom-call | flops 8589934592 | bytes 24117248 | tf_op jit(solution)/shard_map/pallas_call | solution.py:224
  184.5 15.8 %collective-permute-done.19.refs_3_ = bf16[256,2048]{1,0:T(8,128)(2,1)} collective-permute-done((bf16[256,2048]{1,0:T(8,128)(2,1)}, bf16[256,2048]{1,0:T(8,128)(2,1)}, u32[]{:S(2)}, u32[]{:S(2)}) %collective-permute-start.19) | collective-permute-done | bytes 1048608 | tf_op jit(solution)/shard_map/ppermute | solution.py:22
  200.4 3.3 collective-permute-done.22
  219.6 5.0 collective-permute-start.23
  224.6 20.7 %collective-permute-done.27.refs_1_ = bf16[256,2048]{1,0:T(8,128)(2,1)} collective-permute-done((bf16[256,2048]{1,0:T(8,128)(2,1)}, bf16[256,2048]{1,0:T(8,128)(2,1)}, u32[]{:S(2)}, u32[]{:S(2)}) %collective-permute-start.27) | collective-permute-done | bytes 1048608 | tf_op jit(solution)/shard_map/ppermute | solution.py:22
  245.3 22.0 %collective-permute-done.26.refs_7_ = bf16[256,2048]{1,0:T(8,128)(2,1)} collective-permute-done((bf16[256,2048]{1,0:T(8,128)(2,1)}, bf16[256,2048]{1,0:T(8,128)(2,1)}, u32[]{:S(2)}, u32[]{:S(2)}) %collective-permute-start.26) | collective-permute-done | bytes 1048608 | tf_op jit(solution)/shard_map/ppermute | solution.py:22
  268.2 19.8 %shard_map.146 = (bf16[2,1152,2048]{2,1,0:T(8,128)(2,1)}, bf16[2,1152,1024]{2,1,0:T(8,128)(2,1)}) custom-call(f32[8,2,256]{2,1,0:T(2,128)} %copy.96.place, f32[8,2,256]{2,1,0:T(2,128)} %copy.97.weights, bf16[256,2048]{1,0:T(8,128)(2,1)} %bitcast.13.refs_0_, bf16[256,2048]{1,0:T(8,128)(2,1)} %collective-permute-done.4.refs_1_, ...), custom_call_target="tpu_custom_call" | custom-call | flops 12079595520 | bytes 22544384 | tf_op jit(solution)/shard_map/pallas_call | solution.py:405
  297.5 17.0 %collective-permute-done.30.refs_3_ = bf16[256,2048]{1,0:T(8,128)(2,1)} collective-permute-done((bf16[256,2048]{1,0:T(8,128)(2,1)}, bf16[256,2048]{1,0:T(8,128)(2,1)}, u32[]{:S(2)}, u32[]{:S(2)}) %collective-permute-start.30) | collective-permute-done | bytes 1048608 | tf_op jit(solution)/shard_map/ppermute | solution.py:22
  317.6 28.0 %shard_map.147 = (bf16[2,1152,2048]{2,1,0:T(8,128)(2,1)}, bf16[2,1152,1024]{2,1,0:T(8,128)(2,1)}, bf16[2,2,1152,1024]{3,2,1,0:T(8,128)(2,1)}) custom-call(f32[6,2,256]{2,1,0:T(2,128)} %copy.98.place, bf16[256,2048]{1,0:T(8,128)(2,1)} %multiply_convert_fusion.refs_0_, bf16[256,2048]{1,0:T(8,128)(2,1)} %collective-permute-done.27.refs_1_, ...), custom_call_target="tpu_custom_call" | custom-call | flops 16307453952 | bytes 38010880 | tf_op jit(solution)/shard_map/pallas_call | solution.py:451
  345.5 12.6 %collective-permute-done.31.refs_1_ = bf16[256,2048]{1,0:T(8,128)(2,1)} collective-permute-done((bf16[256,2048]{1,0:T(8,128)(2,1)}, bf16[256,2048]{1,0:T(8,128)(2,1)}, u32[]{:S(2)}, u32[]{:S(2)}) %collective-permute-start.31) | collective-permute-done | bytes 1048608 | tf_op jit(solution)/shard_map/ppermute | solution.py:22
  358.8 13.2 %shard_map.148 = (bf16[2,1152,2048]{2,1,0:T(8,128)(2,1)}, bf16[2,1152,1024]{2,1,0:T(8,128)(2,1)}, bf16[2,2,1152,1024]{3,2,1,0:T(8,128)(2,1)}) custom-call(f32[2,2,256]{2,1,0:T(2,128)} %copy.99.place, bf16[256,2048]{1,0:T(8,128)(2,1)} %collective-permute-done.32.refs_0_, ...), custom_call_target="tpu_custom_call", output_to_operand_aliasing={{0}: (6, {}), {1}: (7, {}), {2}: (8, {})} | custom-call | flops 5435817984 | bytes 23855104 | tf_op jit(solution)/shard_map/pallas_call | solution.py:451
  372.7 11.8 %shard_map.149 = (bf16[1,256,2048]{2,1,0:T(8,128)(2,1)}, bf16[1,256,2048]{2,1,0:T(8,128)(2,1)}) custom-call(f32[2,2,256]{2,1,0:T(2,128)} %copy.100.place, f32[2,2,256]{2,1,0:T(2,128)} %copy.101.weights, f32[2,256,2]{2,1,0:T(8,128)} %bitcast.194, bf16[2,2,1152,1024]{3,2,1,0:T(8,128)(2,1)} %get-tuple-element.221.rows.grad_gu, bf16[2,2048,2048]{2,1,0:T(8,128)(2,1)} %weight.4), custom_call_target="tpu_custom_call" | custom-call | flops 5435817984 | bytes 21233664 | tf_op jit(solution)/shard_map/pallas_call | solution.py:515
  388.5 24.7 %shard_map.150 = (bf16[1,256,2048]{2,1,0:T(8,128)(2,1)}, bf16[1,256,2048]{2,1,0:T(8,128)(2,1)}, bf16[1,256,2048]{2,1,0:T(8,128)(2,1)}, bf16[1,256,2048]{2,1,0:T(...) custom-call(f32[6,2,256]{2,1,0:T(2,128)} %copy.102.place, f32[6,2,256]{2,1,0:T(2,128)} %copy.103.weights, ...), custom_call_target="tpu_custom_call" | custom-call | flops 16307453952 | bytes 30146560 | tf_op jit(solution)/shard_map/pallas_call | solution.py:515
  413.2 19.9 %collective-permute-done.33 = bf16[256,2048]{1,0:T(8,128)(2,1)} collective-permute-done((bf16[256,2048]{1,0:T(8,128)(2,1)}, bf16[256,2048]{1,0:T(8,128)(2,1)}, u32[]{:S(2)}, u32[]{:S(2)}) %collective-permute-start.33) | collective-permute-done | bytes 1048608 | tf_op jit(solution)/shard_map/ppermute | solution.py:22
  437.1 24.4 %shard_map.151 = (bf16[2,768,2048]{2,1,0:T(8,128)(2,1)}, bf16[2,768,2048]{2,1,0:T(8,128)(2,1)}) custom-call(s32[1]{0:T(128)} %bitcast.51.me, bf16[2,1152,2048]{2,1,0:T(8,128)(2,1)} %get-tuple-element.219.rows, bf16[2,2,1152,1024]{3,2,1,0:T(8,128)(2,1)} %get-tuple-element.221.rows.grad_gu, bf16[2,1152,1024]{2,1,0:T(8,128)(2,1)} %get-tuple-element.239.activation.rows, ...), custom_call_target="tpu_custom_call" | custom-call | flops 14495514624 | bytes 29097984 | tf_op jit(solution)/shard_map/pallas_call | solution.py:551
  462.6 3.4 fusion.18
  474.4 20.8 %shard_map.152 = (bf16[4,256,2048]{2,1,0:T(8,128)(2,1)}, bf16[4,256,2048]{2,1,0:T(8,128)(2,1)}) custom-call(f32[8,2,256]{2,1,0:T(2,128)} %copy.104.place, f32[8,2,256]{2,1,0:T(2,128)} %copy.97.weights, f32[8,256,2]{2,1,0:T(8,128)} %bitcast.187, bf16[2,1152,1024]{2,1,0:T(8,128)(2,1)} %get-tuple-element.239.activation.rows, bf16[2,1024,2048]{2,1,0:T(8,128)(2,1)} %weight.5), custom_call_target="tpu_custom_call" | custom-call | flops 12079595520 | bytes 21495808 | tf_op jit(solution)/shard_map/pallas_call | solution.py:515
  495.3 22.5 %collective-permute-done.40 = bf16[256,2048]{1,0:T(8,128)(2,1)} collective-permute-done((bf16[256,2048]{1,0:T(8,128)(2,1)}, bf16[256,2048]{1,0:T(8,128)(2,1)}, u32[]{:S(2)}, u32[]{:S(2)}) %collective-permute-start.40) | collective-permute-done | bytes 1048608 | tf_op jit(solution)/shard_map/ppermute | solution.py:22
  520.7 5.0 fusion.40
  528.5 24.2 %shard_map.153 = (bf16[2,768,2048]{2,1,0:T(8,128)(2,1)}, bf16[2,768,2048]{2,1,0:T(8,128)(2,1)}) custom-call(s32[1]{0:T(128)} %bitcast.51.me, bf16[2,1152,2048]{2,1,0:T(8,128)(2,1)} %get-tuple-element.219.rows, bf16[2,2,1152,1024]{3,2,1,0:T(8,128)(2,1)} %get-tuple-element.221.rows.grad_gu, bf16[2,1152,1024]{2,1,0:T(8,128)(2,1)} %get-tuple-element.239.activation.rows, ...), custom_call_target="tpu_custom_call" | custom-call | flops 14495514624 | bytes 29097984 | tf_op jit(solution)/shard_map/pallas_call | solution.py:551
  555.7 3.4 pad_maximum_fusion.1.grad
  559.1 34.3 %shard_map.154 = (bf16[4,256,1536]{2,1,0:T(8,128)(2,1)}, bf16[4,256,2048]{2,1,0:T(8,128)(2,1)}, f32[8,128]{1,0:T(8,128)}, f32[8,2048]{1,0:T(8,128)}) custom-call(s32[4]{0:T(128)} %pad_add_fusion.lens, bf16[4,256,2048]{2,1,0:T(8,128)(2,1)} %pad_maximum_fusion.1.grad, f32[4,256,1536]{2,1,0:T(8,128)} %get-tuple-element.186.proj, ...), custom_call_target="tpu_custom_call" | custom-call | flops 8589934592 | bytes 30408704 | tf_op jit(solution)/shard_map/pallas_call | solution.py:286
  599.8 14.0 %shard_map.155 = bf16[8,4,64,2048]{3,2,1,0:T(8,128)(2,1)} custom-call(s32[1]{0:T(128)} %bitcast.54.me, bf16[1024,2048]{1,0:T(8,128)(2,1)} %bitcast.203, bf16[1024,1536]{1,0:T(8,128)(2,1)} %bitcast.225, bf16[1024,512]{1,0:T(8,128)(2,1)} %bitcast.226, bf16[1024,2048]{1,0:T(8,128)(2,1)} %bitcast.204), custom_call_target="tpu_custom_call" | custom-call | flops 8589934592 | bytes 20971520 | tf_op jit(solution)/shard_map/pallas_call | solution.py:318
  617.0 29.3 %collective-permute-done.38 = bf16[4,256,2048]{2,1,0:T(8,128)(2,1)} collective-permute-done((bf16[4,256,2048]{2,1,0:T(8,128)(2,1)}, bf16[4,256,2048]{2,1,0:T(8,128)(2,1)}, u32[]{:S(2)}, u32[]{:S(2)}) %collective-permute-start.38) | collective-permute-done | bytes 4194336 | tf_op jit(solution)/shard_map/ppermute | solution.py:22
  649.5 4.7 collective-permute-start.46
  654.2 4.2 add_convert_fusion.1
  665.8 3.6 fusion.6
  669.4 16.3 %collective-permute-done.49 = bf16[4,64,2048]{2,1,0:T(8,128)(2,1)S(1)} collective-permute-done((bf16[4,64,2048]{2,1,0:T(8,128)(2,1)S(1)}, bf16[4,64,2048]{2,1,0:T(8,128)(2,1)S(1)}, u32[]{:S(2)}, u32[]{:S(2)}) %collective-permute-start.49) | collective-permute-done | bytes 1048608 | tf_op jit(solution)/shard_map/ppermute | solution.py:22
  685.7 14.1 %collective-permute-done.48 = f32[4352]{0:T(1024)S(1)} collective-permute-done((f32[4352]{0:T(1024)S(1)}, f32[4352]{0:T(1024)S(1)}, u32[]{:S(2)}, u32[]{:S(2)}) %collective-permute-start.48) | collective-permute-done | bytes 17440 | tf_op jit(solution)/shard_map/ppermute | solution.py:22
  709.1 40.6 %collective-permute-done.53 = bf16[1,256,2048]{2,1,0:T(8,128)(2,1)S(1)} collective-permute-done((bf16[1,256,2048]{2,1,0:T(8,128)(2,1)S(1)}, bf16[1,256,2048]{2,1,0:T(8,128)(2,1)S(1)}, u32[]{:S(2)}, u32[]{:S(2)}) %collective-permute-start.53) | collective-permute-done | bytes 1048608 | tf_op jit(solution)/shard_map/ppermute | solution.py:22
  751.2 4.9 add_convert_fusion
  760.8 6.8 shard_map.156
  768.2 7.9 collective-permute-done.57
  779.8 3.4 collective-permute-start.61
  783.3 13.0 %collective-permute-done.56 = bf16[4,64,2048]{2,1,0:T(8,128)(2,1)S(1)} collective-permute-done((bf16[4,64,2048]{2,1,0:T(8,128)(2,1)S(1)}, bf16[4,64,2048]{2,1,0:T(8,128)(2,1)S(1)}, u32[]{:S(2)}, u32[]{:S(2)}) %collective-permute-start.56) | collective-permute-done | bytes 1048608 | tf_op jit(solution)/shard_map/ppermute | solution.py:22
  796.3 27.0 %collective-permute-done.60 = bf16[4,64,2048]{2,1,0:T(8,128)(2,1)S(1)} collective-permute-done((bf16[4,64,2048]{2,1,0:T(8,128)(2,1)S(1)}, bf16[4,64,2048]{2,1,0:T(8,128)(2,1)S(1)}, u32[]{:S(2)}, u32[]{:S(2)}) %collective-permute-start.60) | collective-permute-done | bytes 1048608 | tf_op jit(solution)/shard_map/ppermute | solution.py:22
  831.8 5.3 collective-permute-done.65.refs_1_
  837.1 3.3 collective-permute-done.66.refs_2_
  841.1 3.2 shard_map.157
  844.2 6.7 shard_map.158
  (329 shorter events, 175.1 us)
Async XLA Ops:
  0.7 26.5 %collective-permute-start.4 = (bf16[256,2048]{1,0:T(8,128)(2,1)}, bf16[256,2048]{1,0:T(8,128)(2,1)}, u32[]{:S(2)}, u32[]{:S(2)}) collective-permute-start(bf16[256,2048]{1,0:T(8,128)(2,1)} %bitcast.13.refs_0_), channel_id=1, source_target_pairs={{0,1},{1,0},{2,3},{3,2},{4,5},{5,4},{6,7},{7,6},{8,9},{9,8},{10,11... | collective-permute-start | bytes 3145736 | tf_op jit(solution)/shard_map/ppermute | solution.py:22
  28.6 25.1 %collective-permute-start.11 = (bf16[272,2048]{1,0:T(8,128)(2,1)S(1)}, bf16[272,2048]{1,0:T(8,128)(2,1)S(1)}, u32[]{:S(2)}, u32[]{:S(2)}) collective-permute-start(bf16[272,2048]{1,0:T(8,128)(2,1)S(1)} %fusion.27), channel_id=1, source_target_pairs={{0,1},{1,0},{2,3},{3,2},{4,5},{5,4},{6,7},{7,6},{8,9},{9,8},{10,11... | collective-permute-start | bytes 3342344 | tf_op jit(solution)/shard_map/ppermute | solution.py:22
  29.0 49.0 %collective-permute-start.10 = (bf16[272,2048]{1,0:T(8,128)(2,1)S(1)}, bf16[272,2048]{1,0:T(8,128)(2,1)}, u32[]{:S(2)}, u32[]{:S(2)}) collective-permute-start(bf16[272,2048]{1,0:T(8,128)(2,1)S(1)} %fusion.27), channel_id=1, source_target_pairs={{0,2},{1,3},{2,0},{3,1},{4,6},{5,7},{6,4},{7,5},{8,10},{9,11},{10,... | collective-permute-start | bytes 3342344 | tf_op jit(solution)/shard_map/ppermute | solution.py:22
  30.7 49.5 %collective-permute-start.8 = (bf16[272,2048]{1,0:T(8,128)(2,1)S(1)}, bf16[272,2048]{1,0:T(8,128)(2,1)}, u32[]{:S(2)}, u32[]{:S(2)}) collective-permute-start(bf16[272,2048]{1,0:T(8,128)(2,1)S(1)} %fusion.27), channel_id=1, source_target_pairs={{0,4},{1,5},{2,6},{3,7},{4,0},{5,1},{6,2},{7,3},{8,12},{9,13},{10,... | collective-permute-start | bytes 3342344 | tf_op jit(solution)/shard_map/ppermute | solution.py:22
  40.9 38.4 %collective-permute-start.9 = (bf16[256,2048]{1,0:T(8,128)(2,1)S(1)}, bf16[256,2048]{1,0:T(8,128)(2,1)S(1)}, u32[]{:S(2)}, u32[]{:S(2)}) collective-permute-start(bf16[256,2048]{1,0:T(8,128)(2,1)S(1)} %fusion.3), channel_id=1, source_target_pairs={{0,16},{8,24},{16,0},{24,8},{1,17},{9,25},{17,1},{25,9},{2,18},{10... | collective-permute-start | bytes 3145736 | tf_op jit(solution)/shard_map/ppermute | solution.py:22
  78.0 27.8 %collective-permute-start.15 = (bf16[272,2048]{1,0:T(8,128)(2,1)}, bf16[272,2048]{1,0:T(8,128)(2,1)}, u32[]{:S(2)}, u32[]{:S(2)}) collective-permute-start(bf16[272,2048]{1,0:T(8,128)(2,1)} %collective-permute-done.10), channel_id=1, source_target_pairs={{0,1},{1,0},{2,3},{3,2},{4,5},{5,4},{6,7},{7,6},{8,9},{9,8},{10,11... | collective-permute-start | bytes 3342344 | tf_op jit(solution)/shard_map/ppermute | solution.py:22
  80.3 46.2 %collective-permute-start.17 = (bf16[272,2048]{1,0:T(8,128)(2,1)}, bf16[272,2048]{1,0:T(8,128)(2,1)S(1)}, u32[]{:S(2)}, u32[]{:S(2)}) collective-permute-start(bf16[272,2048]{1,0:T(8,128)(2,1)} %collective-permute-done.8), channel_id=1, source_target_pairs={{0,1},{1,0},{2,3},{3,2},{4,5},{5,4},{6,7},{7,6},{8,9},{9,8},{10,11... | collective-permute-start | bytes 3342344 | tf_op jit(solution)/shard_map/ppermute | solution.py:22
  81.8 25.4 %collective-permute-start.13 = (bf16[272,2048]{1,0:T(8,128)(2,1)}, bf16[272,2048]{1,0:T(8,128)(2,1)}, u32[]{:S(2)}, u32[]{:S(2)}) collective-permute-start(bf16[272,2048]{1,0:T(8,128)(2,1)} %collective-permute-done.8), channel_id=1, source_target_pairs={{0,2},{1,3},{2,0},{3,1},{4,6},{5,7},{6,4},{7,5},{8,10},{9,11},{10,... | collective-permute-start | bytes 3342344 | tf_op jit(solution)/shard_map/ppermute | solution.py:22
  129.4 45.7 %collective-permute-start.21 = (bf16[256,2048]{1,0:T(8,128)(2,1)}, bf16[256,2048]{1,0:T(8,128)(2,1)}, u32[]{:S(2)}, u32[]{:S(2)}) collective-permute-start(bf16[256,2048]{1,0:T(8,128)(2,1)} %bitcast.13.refs_0_), channel_id=1, source_target_pairs={{0,4},{1,5},{2,6},{3,7},{4,0},{5,1},{6,2},{7,3},{8,12},{9,13},{10,... | collective-permute-start | bytes 3145736 | tf_op jit(solution)/shard_map/ppermute | solution.py:22
  174.0 26.3 %collective-permute-start.19 = (bf16[256,2048]{1,0:T(8,128)(2,1)}, bf16[256,2048]{1,0:T(8,128)(2,1)}, u32[]{:S(2)}, u32[]{:S(2)}) collective-permute-start(bf16[256,2048]{1,0:T(8,128)(2,1)} %collective-permute-done.3.refs_2_), channel_id=1, source_target_pairs={{0,1},{1,0},{2,3},{3,2},{4,5},{5,4},{6,7},{7,6},{8,9},{9,8},{10,11... | collective-permute-start | bytes 3145736 | tf_op jit(solution)/shard_map/ppermute | solution.py:22
  175.1 25.2 %collective-permute-start.18 = (bf16[256,2048]{1,0:T(8,128)(2,1)}, bf16[256,2048]{1,0:T(8,128)(2,1)}, u32[]{:S(2)}, u32[]{:S(2)}) collective-permute-start(bf16[256,2048]{1,0:T(8,128)(2,1)} %get-tuple-element.334), channel_id=1, source_target_pairs={{0,8},{8,0},{16,24},{24,16},{1,9},{9,1},{17,25},{25,17},{2,10},{10... | collective-permute-start | bytes 3145736 | tf_op jit(solution)/shard_map/ppermute | solution.py:22
  178.3 25.4 %collective-permute-start.22 = (bf16[256,2048]{1,0:T(8,128)(2,1)S(1)}, bf16[256,2048]{1,0:T(8,128)(2,1)}, u32[]{:S(2)}, u32[]{:S(2)}) collective-permute-start(bf16[256,2048]{1,0:T(8,128)(2,1)S(1)} %fusion.23), channel_id=1, source_target_pairs={{0,16},{8,24},{16,0},{24,8},{1,17},{9,25},{17,1},{25,9},{2,18},{10... | collective-permute-start | bytes 3145736 | tf_op jit(solution)/shard_map/ppermute | solution.py:22
  183.0 41.6 %collective-permute-start.28 = (bf16[256,2048]{1,0:T(8,128)(2,1)}, bf16[256,2048]{1,0:T(8,128)(2,1)}, u32[]{:S(2)}, u32[]{:S(2)}) collective-permute-start(bf16[256,2048]{1,0:T(8,128)(2,1)} %collective-permute-done.21.refs_4_), channel_id=1, source_target_pairs={{0,1},{1,0},{2,3},{3,2},{4,5},{5,4},{6,7},{7,6},{8,9},{9,8},{10,11... | collective-permute-start | bytes 3145736 | tf_op jit(solution)/shard_map/ppermute | solution.py:22
  207.5 37.8 %collective-permute-start.27 = (bf16[256,2048]{1,0:T(8,128)(2,1)}, bf16[256,2048]{1,0:T(8,128)(2,1)}, u32[]{:S(2)}, u32[]{:S(2)}) collective-permute-start(bf16[256,2048]{1,0:T(8,128)(2,1)} %multiply_convert_fusion.refs_0_), channel_id=1, source_target_pairs={{0,1},{1,0},{2,3},{3,2},{4,5},{5,4},{6,7},{7,6},{8,9},{9,8},{10,11... | collective-permute-start | bytes 3145736 | tf_op jit(solution)/shard_map/ppermute | solution.py:22
  209.5 57.8 %collective-permute-start.26 = (bf16[256,2048]{1,0:T(8,128)(2,1)}, bf16[256,2048]{1,0:T(8,128)(2,1)}, u32[]{:S(2)}, u32[]{:S(2)}) collective-permute-start(bf16[256,2048]{1,0:T(8,128)(2,1)} %collective-permute-done.25.refs_5_), channel_id=1, source_target_pairs={{0,1},{1,0},{2,3},{3,2},{4,5},{5,4},{6,7},{7,6},{8,9},{9,8},{10,11... | collective-permute-start | bytes 3145736 | tf_op jit(solution)/shard_map/ppermute | solution.py:22
  219.3 68.8 %collective-permute-start.24 = (bf16[256,2048]{1,0:T(8,128)(2,1)}, bf16[256,2048]{1,0:T(8,128)(2,1)}, u32[]{:S(2)}, u32[]{:S(2)}) collective-permute-start(bf16[256,2048]{1,0:T(8,128)(2,1)} %multiply_convert_fusion.refs_0_), channel_id=1, source_target_pairs={{0,2},{1,3},{2,0},{3,1},{4,6},{5,7},{6,4},{7,5},{8,10},{9,11},{10,... | collective-permute-start | bytes 3145736 | tf_op jit(solution)/shard_map/ppermute | solution.py:22
  219.6 69.6 %collective-permute-start.23 = (bf16[256,2048]{1,0:T(8,128)(2,1)}, bf16[256,2048]{1,0:T(8,128)(2,1)}, u32[]{:S(2)}, u32[]{:S(2)}) collective-permute-start(bf16[256,2048]{1,0:T(8,128)(2,1)} %multiply_convert_fusion.refs_0_), channel_id=1, source_target_pairs={{0,4},{1,5},{2,6},{3,7},{4,0},{5,1},{6,2},{7,3},{8,12},{9,13},{10,... | collective-permute-start | bytes 3145736 | tf_op jit(solution)/shard_map/ppermute | solution.py:22
  288.1 26.5 %collective-permute-start.30 = (bf16[256,2048]{1,0:T(8,128)(2,1)}, bf16[256,2048]{1,0:T(8,128)(2,1)}, u32[]{:S(2)}, u32[]{:S(2)}) collective-permute-start(bf16[256,2048]{1,0:T(8,128)(2,1)} %collective-permute-done.24.refs_2_), channel_id=1, source_target_pairs={{0,1},{1,0},{2,3},{3,2},{4,5},{5,4},{6,7},{7,6},{8,9},{9,8},{10,11... | collective-permute-start | bytes 3145736 | tf_op jit(solution)/shard_map/ppermute | solution.py:22
  289.2 25.3 %collective-permute-start.29 = (bf16[256,2048]{1,0:T(8,128)(2,1)}, bf16[256,2048]{1,0:T(8,128)(2,1)}, u32[]{:S(2)}, u32[]{:S(2)}) collective-permute-start(bf16[256,2048]{1,0:T(8,128)(2,1)} %collective-permute-done.23.refs_4_), channel_id=1, source_target_pairs={{0,2},{1,3},{2,0},{3,1},{4,6},{5,7},{6,4},{7,5},{8,10},{9,11},{10,... | collective-permute-start | bytes 3145736 | tf_op jit(solution)/shard_map/ppermute | solution.py:22
  296.5 49.0 %collective-permute-start.32 = (bf16[256,2048]{1,0:T(8,128)(2,1)}, bf16[256,2048]{1,0:T(8,128)(2,1)}, u32[]{:S(2)}, u32[]{:S(2)}) collective-permute-start(bf16[256,2048]{1,0:T(8,128)(2,1)} %collective-permute-done.23.refs_4_), channel_id=1, source_target_pairs={{0,1},{1,0},{2,3},{3,2},{4,5},{5,4},{6,7},{7,6},{8,9},{9,8},{10,11... | collective-permute-start | bytes 3145736 | tf_op jit(solution)/shard_map/ppermute | solution.py:22
  314.5 43.6 %collective-permute-start.31 = (bf16[256,2048]{1,0:T(8,128)(2,1)}, bf16[256,2048]{1,0:T(8,128)(2,1)}, u32[]{:S(2)}, u32[]{:S(2)}) collective-permute-start(bf16[256,2048]{1,0:T(8,128)(2,1)} %collective-permute-done.29.refs_5_), channel_id=1, source_target_pairs={{0,1},{1,0},{2,3},{3,2},{4,5},{5,4},{6,7},{7,6},{8,9},{9,8},{10,11... | collective-permute-start | bytes 3145736 | tf_op jit(solution)/shard_map/ppermute | solution.py:22
  386.5 75.0 %collective-permute-start.36 = (bf16[256,2048]{1,0:T(8,128)(2,1)}, bf16[256,2048]{1,0:T(8,128)(2,1)}, u32[]{:S(2)}, u32[]{:S(2)}) collective-permute-start(bf16[256,2048]{1,0:T(8,128)(2,1)} %bitcast.223), channel_id=1, source_target_pairs={{0,1},{1,0},{2,3},{3,2},{4,5},{5,4},{6,7},{7,6},{8,9},{9,8},{10,11... | collective-permute-start | bytes 3145736 | tf_op jit(solution)/shard_map/ppermute | solution.py:22
  387.6 45.5 %collective-permute-start.33 = (bf16[256,2048]{1,0:T(8,128)(2,1)}, bf16[256,2048]{1,0:T(8,128)(2,1)}, u32[]{:S(2)}, u32[]{:S(2)}) collective-permute-start(bf16[256,2048]{1,0:T(8,128)(2,1)} %bitcast.224), channel_id=1, source_target_pairs={{0,1},{1,0},{2,3},{3,2},{4,5},{5,4},{6,7},{7,6},{8,9},{9,8},{10,11... | collective-permute-start | bytes 3145736 | tf_op jit(solution)/shard_map/ppermute | solution.py:22
  436.1 29.9 %collective-permute-start.34 = (bf16[256,2048]{1,0:T(8,128)(2,1)}, bf16[256,2048]{1,0:T(8,128)(2,1)}, u32[]{:S(2)}, u32[]{:S(2)}) collective-permute-start(bf16[256,2048]{1,0:T(8,128)(2,1)} %bitcast.47), channel_id=1, source_target_pairs={{0,1},{1,0},{2,3},{3,2},{4,5},{5,4},{6,7},{7,6},{8,9},{9,8},{10,11... | collective-permute-start | bytes 3145736 | tf_op jit(solution)/shard_map/ppermute | solution.py:22
  437.1 25.5 %collective-permute-start.35 = (bf16[256,2048]{1,0:T(8,128)(2,1)}, bf16[256,2048]{1,0:T(8,128)(2,1)}, u32[]{:S(2)}, u32[]{:S(2)}) collective-permute-start(bf16[256,2048]{1,0:T(8,128)(2,1)} %fusion.22), channel_id=1, source_target_pairs={{0,2},{1,3},{2,0},{3,1},{4,6},{5,7},{6,4},{7,5},{8,10},{9,11},{10,... | collective-permute-start | bytes 3145736 | tf_op jit(solution)/shard_map/ppermute | solution.py:22
  461.5 97.5 %collective-permute-start.39 = (bf16[2,768,2048]{2,1,0:T(8,128)(2,1)}, bf16[2,768,2048]{2,1,0:T(8,128)(2,1)}, u32[]{:S(2)}, u32[]{:S(2)}) collective-permute-start(bf16[2,768,2048]{2,1,0:T(8,128)(2,1)} %get-tuple-element.242), channel_id=1, source_target_pairs={{0,8},{8,0},{16,24},{24,16},{1,9},{9,1},{17,25},{25,17},{2,10},{10... | collective-permute-start | bytes 18874376 | tf_op jit(solution)/shard_map/ppermute | solution.py:22
  461.5 33.7 %collective-permute-start.37 = (bf16[256,2048]{1,0:T(8,128)(2,1)}, bf16[256,2048]{1,0:T(8,128)(2,1)}, u32[]{:S(2)}, u32[]{:S(2)}) collective-permute-start(bf16[256,2048]{1,0:T(8,128)(2,1)} %bitcast.222), channel_id=1, source_target_pairs={{0,1},{1,0},{2,3},{3,2},{4,5},{5,4},{6,7},{7,6},{8,9},{9,8},{10,11... | collective-permute-start | bytes 3145736 | tf_op jit(solution)/shard_map/ppermute | solution.py:22
  469.5 48.3 %collective-permute-start.40 = (bf16[256,2048]{1,0:T(8,128)(2,1)}, bf16[256,2048]{1,0:T(8,128)(2,1)}, u32[]{:S(2)}, u32[]{:S(2)}) collective-permute-start(bf16[256,2048]{1,0:T(8,128)(2,1)} %fusion.19), channel_id=1, source_target_pairs={{0,2},{1,3},{2,0},{3,1},{4,6},{5,7},{6,4},{7,5},{8,10},{9,11},{10,... | collective-permute-start | bytes 3145736 | tf_op jit(solution)/shard_map/ppermute | solution.py:22
  471.5 46.3 %collective-permute-start.41 = (bf16[256,2048]{1,0:T(8,128)(2,1)}, bf16[256,2048]{1,0:T(8,128)(2,1)}, u32[]{:S(2)}, u32[]{:S(2)}) collective-permute-start(bf16[256,2048]{1,0:T(8,128)(2,1)} %fusion.18), channel_id=1, source_target_pairs={{0,4},{1,5},{2,6},{3,7},{4,0},{5,1},{6,2},{7,3},{8,12},{9,13},{10,... | collective-permute-start | bytes 3145736 | tf_op jit(solution)/shard_map/ppermute | solution.py:22
  525.7 27.1 %collective-permute-start.42 = (bf16[256,2048]{1,0:T(8,128)(2,1)}, bf16[256,2048]{1,0:T(8,128)(2,1)}, u32[]{:S(2)}, u32[]{:S(2)}) collective-permute-start(bf16[256,2048]{1,0:T(8,128)(2,1)} %get-tuple-element.259), channel_id=1, source_target_pairs={{0,16},{8,24},{16,0},{24,8},{1,17},{9,25},{17,1},{25,9},{2,18},{10... | collective-permute-start | bytes 3145736 | tf_op jit(solution)/shard_map/ppermute | solution.py:22
  552.9 93.4 %collective-permute-start.38 = (bf16[4,256,2048]{2,1,0:T(8,128)(2,1)}, bf16[4,256,2048]{2,1,0:T(8,128)(2,1)}, u32[]{:S(2)}, u32[]{:S(2)}) collective-permute-start(bf16[4,256,2048]{2,1,0:T(8,128)(2,1)} %get-tuple-element.254), channel_id=1, source_target_pairs={{0,1},{1,0},{2,3},{3,2},{4,5},{5,4},{6,7},{7,6},{8,9},{9,8},{10,11... | collective-permute-start | bytes 12582920 | tf_op jit(solution)/shard_map/ppermute | solution.py:22
  554.0 107.8 %collective-permute-start.51 = (bf16[2,768,2048]{2,1,0:T(8,128)(2,1)}, bf16[2,768,2048]{2,1,0:T(8,128)(2,1)}, u32[]{:S(2)}, u32[]{:S(2)}) collective-permute-start(bf16[2,768,2048]{2,1,0:T(8,128)(2,1)} %get-tuple-element.264), channel_id=1, source_target_pairs={{0,8},{8,0},{16,24},{24,16},{1,9},{9,1},{17,25},{25,17},{2,10},{10... | collective-permute-start | bytes 18874376 | tf_op jit(solution)/shard_map/ppermute | solution.py:22
  598.5 59.9 %collective-permute-start.47 = (f32[4352]{0:T(1024)S(1)}, f32[4352]{0:T(1024)S(1)}, u32[]{:S(2)}, u32[]{:S(2)}) collective-permute-start(f32[4352]{0:T(1024)S(1)} %pad_maximum_fusion.8), channel_id=1, source_target_pairs={{0,1},{1,0},{2,3},{3,2},{4,5},{5,4},{6,7},{7,6},{8,9},{9,8},{10,11... | collective-permute-start | bytes 52232 | tf_op jit(solution)/shard_map/ppermute | solution.py:22
  599.7 63.6 %collective-permute-start.50 = (bf16[256,2048]{1,0:T(8,128)(2,1)}, bf16[256,2048]{1,0:T(8,128)(2,1)}, u32[]{:S(2)}, u32[]{:S(2)}) collective-permute-start(bf16[256,2048]{1,0:T(8,128)(2,1)} %get-tuple-element.332), channel_id=1, source_target_pairs={{0,8},{8,0},{16,24},{24,16},{1,9},{9,1},{17,25},{25,17},{2,10},{10... | collective-permute-start | bytes 3145736 | tf_op jit(solution)/shard_map/ppermute | solution.py:22
  615.4 48.1 %collective-permute-start.52 = (bf16[256,2048]{1,0:T(8,128)(2,1)S(1)}, bf16[256,2048]{1,0:T(8,128)(2,1)S(1)}, u32[]{:S(2)}, u32[]{:S(2)}) collective-permute-start(bf16[256,2048]{1,0:T(8,128)(2,1)S(1)} %fusion.14), channel_id=1, source_target_pairs={{0,16},{8,24},{16,0},{24,8},{1,17},{9,25},{17,1},{25,9},{2,18},{10... | collective-permute-start | bytes 3145736 | tf_op jit(solution)/shard_map/ppermute | solution.py:22
  649.5 50.3 %collective-permute-start.46 = (bf16[2,256,2048]{2,1,0:T(8,128)(2,1)S(1)}, bf16[2,256,2048]{2,1,0:T(8,128)(2,1)S(1)}, u32[]{:S(2)}, u32[]{:S(2)}) collective-permute-start(bf16[2,256,2048]{2,1,0:T(8,128)(2,1)S(1)} %add_convert_fusion.2), channel_id=1, source_target_pairs={{0,2},{1,3},{2,0},{3,1},{4,6},{5,7},{6,4},{7,5},{8,10},{9,11},{10,... | collective-permute-start | bytes 6291464 | tf_op jit(solution)/shard_map/ppermute | solution.py:22
  658.4 102.3 %collective-permute-start.59 = (bf16[1,768,2048]{2,1,0:T(8,128)(2,1)S(1)}, bf16[1,768,2048]{2,1,0:T(8,128)(2,1)}, u32[]{:S(2)}, u32[]{:S(2)}) collective-permute-start(bf16[1,768,2048]{2,1,0:T(8,128)(2,1)S(1)} %add_convert_fusion.1), channel_id=1, source_target_pairs={{0,16},{8,24},{16,0},{24,8},{1,17},{9,25},{17,1},{25,9},{2,18},{10... | collective-permute-start | bytes 9437192 | tf_op jit(solution)/shard_map/ppermute | solution.py:22
  663.3 36.5 %collective-permute-start.48 = (f32[4352]{0:T(1024)S(1)}, f32[4352]{0:T(1024)S(1)}, u32[]{:S(2)}, u32[]{:S(2)}) collective-permute-start(f32[4352]{0:T(1024)S(1)} %fusion.39), channel_id=1, source_target_pairs={{0,2},{1,3},{2,0},{3,1},{4,6},{5,7},{6,4},{7,5},{8,10},{9,11},{10,... | collective-permute-start | bytes 52232 | tf_op jit(solution)/shard_map/ppermute | solution.py:22
  701.6 48.1 %collective-permute-start.53 = (bf16[1,256,2048]{2,1,0:T(8,128)(2,1)S(1)}, bf16[1,256,2048]{2,1,0:T(8,128)(2,1)S(1)}, u32[]{:S(2)}, u32[]{:S(2)}) collective-permute-start(bf16[1,256,2048]{2,1,0:T(8,128)(2,1)S(1)} %add_convert_fusion.3), channel_id=1, source_target_pairs={{0,4},{1,5},{2,6},{3,7},{4,0},{5,1},{6,2},{7,3},{8,12},{9,13},{10,... | collective-permute-start | bytes 3145736 | tf_op jit(solution)/shard_map/ppermute | solution.py:22
  704.3 56.4 %collective-permute-start.54 = (bf16[4,64,2048]{2,1,0:T(8,128)(2,1)}, bf16[4,64,2048]{2,1,0:T(8,128)(2,1)S(1)}, u32[]{:S(2)}, u32[]{:S(2)}) collective-permute-start(bf16[4,64,2048]{2,1,0:T(8,128)(2,1)} %get-tuple-element.328), channel_id=1, source_target_pairs={{0,1},{1,0},{2,3},{3,2},{4,5},{5,4},{6,7},{7,6},{8,9},{9,8},{10,11... | collective-permute-start | bytes 3145736 | tf_op jit(solution)/shard_map/ppermute | solution.py:22
  705.8 50.3 %collective-permute-start.55 = (f32[4352]{0:T(1024)S(1)}, f32[4352]{0:T(1024)S(1)}, u32[]{:S(2)}, u32[]{:S(2)}) collective-permute-start(f32[4352]{0:T(1024)S(1)} %add.344), channel_id=1, source_target_pairs={{0,4},{1,5},{2,6},{3,7},{4,0},{5,1},{6,2},{7,3},{8,12},{9,13},{10,... | collective-permute-start | bytes 52232 | tf_op jit(solution)/shard_map/ppermute | solution.py:22
  707.4 60.2 %collective-permute-start.58 = (bf16[4,64,2048]{2,1,0:T(8,128)(2,1)}, bf16[4,64,2048]{2,1,0:T(8,128)(2,1)}, u32[]{:S(2)}, u32[]{:S(2)}) collective-permute-start(bf16[4,64,2048]{2,1,0:T(8,128)(2,1)} %fusion.11), channel_id=1, source_target_pairs={{0,2},{1,3},{2,0},{3,1},{4,6},{5,7},{6,4},{7,5},{8,10},{9,11},{10,... | collective-permute-start | bytes 3145736 | tf_op jit(solution)/shard_map/ppermute | solution.py:22
  749.7 26.4 %collective-permute-start.57 = (bf16[4,64,2048]{2,1,0:T(8,128)(2,1)}, bf16[4,64,2048]{2,1,0:T(8,128)(2,1)}, u32[]{:S(2)}, u32[]{:S(2)}) collective-permute-start(bf16[4,64,2048]{2,1,0:T(8,128)(2,1)} %get-tuple-element.296), channel_id=1, source_target_pairs={{0,1},{1,0},{2,3},{3,2},{4,5},{5,4},{6,7},{7,6},{8,9},{9,8},{10,11... | collective-permute-start | bytes 3145736 | tf_op jit(solution)/shard_map/ppermute | solution.py:22
  756.1 88.2 %collective-permute-start.67 = (bf16[1,768,2048]{2,1,0:T(8,128)(2,1)}, bf16[1,768,2048]{2,1,0:T(8,128)(2,1)}, u32[]{:S(2)}, u32[]{:S(2)}) collective-permute-start(bf16[1,768,2048]{2,1,0:T(8,128)(2,1)} %add_convert_fusion), channel_id=1, source_target_pairs={{0,16},{8,24},{16,0},{24,8},{1,17},{9,25},{17,1},{25,9},{2,18},{10... | collective-permute-start | bytes 9437192 | tf_op jit(solution)/shard_map/ppermute | solution.py:22
  767.6 28.7 %collective-permute-start.56 = (bf16[4,64,2048]{2,1,0:T(8,128)(2,1)S(1)}, bf16[4,64,2048]{2,1,0:T(8,128)(2,1)S(1)}, u32[]{:S(2)}, u32[]{:S(2)}) collective-permute-start(bf16[4,64,2048]{2,1,0:T(8,128)(2,1)S(1)} %copy-done.21), channel_id=1, source_target_pairs={{0,1},{1,0},{2,3},{3,2},{4,5},{5,4},{6,7},{7,6},{8,9},{9,8},{10,11... | collective-permute-start | bytes 3145736 | tf_op jit(solution)/shard_map/ppermute | solution.py:22
  779.3 44.0 %collective-permute-start.60 = (bf16[4,64,2048]{2,1,0:T(8,128)(2,1)S(1)}, bf16[4,64,2048]{2,1,0:T(8,128)(2,1)S(1)}, u32[]{:S(2)}, u32[]{:S(2)}) collective-permute-start(bf16[4,64,2048]{2,1,0:T(8,128)(2,1)S(1)} %get-tuple-element.330), channel_id=1, source_target_pairs={{0,2},{1,3},{2,0},{3,1},{4,6},{5,7},{6,4},{7,5},{8,10},{9,11},{10,... | collective-permute-start | bytes 3145736 | tf_op jit(solution)/shard_map/ppermute | solution.py:22
  779.8 47.3 %collective-permute-start.61 = (bf16[4,64,2048]{2,1,0:T(8,128)(2,1)S(1)}, bf16[4,64,2048]{2,1,0:T(8,128)(2,1)S(1)}, u32[]{:S(2)}, u32[]{:S(2)}) collective-permute-start(bf16[4,64,2048]{2,1,0:T(8,128)(2,1)S(1)} %get-tuple-element.331), channel_id=1, source_target_pairs={{0,4},{1,5},{2,6},{3,7},{4,0},{5,1},{6,2},{7,3},{8,12},{9,13},{10,... | collective-permute-start | bytes 3145736 | tf_op jit(solution)/shard_map/ppermute | solution.py:22
  783.3 40.0 %collective-permute-start.62 = (f32[4352]{0:T(1024)S(1)}, f32[4352]{0:T(1024)S(1)}, u32[]{:S(2)}, u32[]{:S(2)}) collective-permute-start(f32[4352]{0:T(1024)S(1)} %add.352), channel_id=1, source_target_pairs={{0,8},{8,0},{16,24},{24,16},{1,9},{9,1},{17,25},{25,17},{2,10},{10... | collective-permute-start | bytes 52232 | tf_op jit(solution)/shard_map/ppermute | solution.py:22
  (66 other events, 1134.6 us)
